TPU v7x, 32 devices: a whole 2x2x4 slice. The times are simulated.
32 devices in a mesh: section: 2 (over x), dp: 4 (over y, core), inner: 4 (over z).
Axes of the slice: x: 2, y: 2, z: 4, core: 2. Of those that a mesh axis runs over, the one named last changes fastest.
Arguments:
- block_io: bfloat16 [2, 32, 320, 768], P('section', ('dp', 'inner')), may hold values from -6 to 6
- segments: int32 [32, 320], P(('dp', 'inner')), may hold values from 0 to 5, as said below
- valid_tokens: int32 [32, 320], P(('dp', 'inner')), may hold values from 0 to 1, as said below
- attention_gain: bfloat16 [2, 768], P('section'), may hold values from 0.5 to 1.5
- attention_shift: bfloat16 [2, 768], P('section'), may hold values from -3 to 3
- triple_weight: bfloat16 [2, 768, 2304], P('section'), may hold values from -0.21875 to 0.21875
- triple_bias: bfloat16 [2, 1536], P('section'), may hold values from -3 to 3
- output_weight: bfloat16 [2, 768, 768], P('section'), may hold values from -1.75 to 1.75
- output_bias: bfloat16 [2, 768], P('section'), may hold values from -3 to 3
- attention_scale: bfloat16 [2, 768], P('section'), may hold values from 0.5 to 1.5
- feed_gain: bfloat16 [2, 768], P('section'), may hold values from 0.5 to 1.5
- feed_shift: bfloat16 [2, 768], P('section'), may hold values from -3 to 3
- up_weight: bfloat16 [2, 768, 3072], P('section'), may hold values from -0.21875 to 0.21875
- up_bias: bfloat16 [2, 3072], P('section'), may hold values from -3 to 3
- down_weight: bfloat16 [2, 3072, 768], P('section'), may hold values from -0.109375 to 0.109375
- down_bias: bfloat16 [2, 768], P('section'), may hold values from -3 to 3
- feed_scale: bfloat16 [2, 768], P('section'), may hold values from 0.5 to 1.5
Outputs:
- block_ends: float32 [2, 32, 320, 768], P('section', ('dp', 'inner'))
- grad_attention_gain: float32 [2, 768], P('section')
- grad_attention_shift: float32 [2, 768], P('section')
- grad_triple_weight: float32 [2, 768, 2304], P('section')
- grad_triple_bias: float32 [2, 1536], P('section')
- grad_output_weight: float32 [2, 768, 768], P('section')
- grad_output_bias: float32 [2, 768], P('section')
- grad_attention_scale: float32 [2, 768], P('section')
- grad_feed_gain: float32 [2, 768], P('section')
- grad_feed_shift: float32 [2, 768], P('section')
- grad_up_weight: float32 [2, 768, 3072], P('section')
- grad_up_bias: float32 [2, 3072], P('section')
- grad_down_weight: float32 [2, 3072, 768], P('section')
- grad_down_bias: float32 [2, 768], P('section')
- grad_feed_scale: float32 [2, 768], P('section')
Inputs may be any that keep to these rules, and one draw needn't show every extreme that they name: `segments`: along a packed sequence the segment ids number its images from 0 upward and never fall; padding follows all images of its sequence and carries the id after the last image's. valid_tokens is 1 on image tokens and 0 on the padding at a sequence's end; every sequence starts with an image.
All inputs are finite; a program needn't handle non-finite values.
Results may differ from a plain program's by a relative error of at most 0.0075.
Values may be sent and summed in bfloat16 or wider, within the bound.
A program may use at most 192 MiB of HBM per device.

v0:
```python
import jax
import jax.numpy as jnp
from jax import lax
from jax.sharding import PartitionSpec as P

HEADS = 12
HEAD = 64
MB = 2
SPM = 1


def passed_along(value, axis, steps):
    count = lax.axis_size(axis)
    first, last = (max(0, -steps), min(count, count - steps))
    return lax.ppermute(value, axis, [(source, source + steps) for source in range(first, last)])


def layer_norm(values, gain, shift):
    center = values - jnp.mean(values, axis=-1, keepdims=True)
    spread = jnp.mean(center * center, axis=-1, keepdims=True)
    return center * lax.rsqrt(spread + 1e-06) * gain + shift


def gelu_exact(values):
    return jax.nn.gelu(values, approximate=False)


def attention_mask(segment_rows, valid_rows):
    same = segment_rows[:, :, None] == segment_rows[:, None, :]
    usable = same & (valid_rows[:, None, :] == 1)
    places = jnp.arange(segment_rows.shape[1], dtype=jnp.int32)
    return usable | (places[:, None] == places[None, :])[None]


def micro_rows(array, index, count):
    return lax.dynamic_slice_in_dim(array, index * count, count, 0)


def attention_scores(triple, allowed, count, length):
    width = triple.shape[1] // 3
    query_part = triple[:, :width].reshape(count, length, HEADS, HEAD)
    key_part = triple[:, width : 2 * width].reshape(count, length, HEADS, HEAD)
    value_part = triple[:, 2 * width :].reshape(count, length, HEADS, HEAD)
    scores = jnp.einsum(
        "bqhd,bkhd->bhqk", query_part, key_part, preferred_element_type=jnp.float32
    ) * HEAD ** (-0.5)
    scores = jnp.where(allowed[:, None], scores, -1000000000.0)
    return (scores, query_part, key_part, value_part)


def block_forward(section_input, params, allowed):
    (
        attention_gain,
        attention_shift,
        triple_weight,
        triple_bias,
        output_weight,
        output_bias,
        attention_scale,
        feed_gain,
        feed_shift,
        up_weight,
        up_bias,
        down_weight,
        down_bias,
        feed_scale,
    ) = params
    count, length, width = section_input.shape
    block_in = section_input.astype(jnp.float32).reshape(count * length, width)
    normed = layer_norm(
        block_in, attention_gain.astype(jnp.float32), attention_shift.astype(jnp.float32)
    ).astype(jnp.bfloat16)
    bias_row = triple_bias.astype(jnp.float32)
    triple_shift = jnp.concatenate(
        [bias_row[:width], jnp.zeros((width,), jnp.float32), bias_row[width:]]
    )
    triple = (
        jnp.dot(normed, triple_weight, preferred_element_type=jnp.float32) + triple_shift
    ).astype(jnp.bfloat16)
    scores, query_part, key_part, value_part = attention_scores(triple, allowed, count, length)
    highest = jnp.max(scores, axis=-1, keepdims=True)
    exponent = jnp.exp(scores - highest)
    totals = jnp.sum(exponent, axis=-1, keepdims=True)
    log_total = highest + jnp.log(totals)
    probabilities = (exponent / totals).astype(jnp.bfloat16)
    attended = jnp.einsum(
        "bhqk,bkhd->bqhd", probabilities, value_part, preferred_element_type=jnp.float32
    )
    attended = attended.astype(jnp.bfloat16).reshape(count * length, width)
    branch_one = jnp.dot(
        attended, output_weight, preferred_element_type=jnp.float32
    ) + output_bias.astype(jnp.float32)
    midway = block_in + attention_scale.astype(jnp.float32) * branch_one
    normed_two = layer_norm(
        midway, feed_gain.astype(jnp.float32), feed_shift.astype(jnp.float32)
    ).astype(jnp.bfloat16)
    hidden_pre = jnp.dot(
        normed_two, up_weight, preferred_element_type=jnp.float32
    ) + up_bias.astype(jnp.float32)
    hidden = gelu_exact(hidden_pre).astype(jnp.bfloat16)
    branch_two = jnp.dot(
        hidden, down_weight, preferred_element_type=jnp.float32
    ) + down_bias.astype(jnp.float32)
    result = midway + feed_scale.astype(jnp.float32) * branch_two
    stored = (
        block_in,
        normed,
        triple,
        log_total,
        attended,
        branch_one,
        midway,
        normed_two,
        hidden_pre,
        hidden,
        branch_two,
    )
    return (result, stored)


def block_backward(stored, upstream, params, allowed, count, length):
    (
        attention_gain,
        attention_shift,
        triple_weight,
        triple_bias,
        output_weight,
        output_bias,
        attention_scale,
        feed_gain,
        feed_shift,
        up_weight,
        up_bias,
        down_weight,
        down_bias,
        feed_scale,
    ) = params
    (
        block_in,
        normed,
        triple,
        log_total,
        attended,
        branch_one,
        midway,
        normed_two,
        hidden_pre,
        hidden,
        branch_two,
    ) = stored
    width = block_in.shape[1]
    grad_feed_scale = jnp.sum(upstream * branch_two, axis=0)
    grad_branch_two = (upstream * feed_scale.astype(jnp.float32)).astype(jnp.bfloat16)
    grad_down_bias = jnp.sum(grad_branch_two.astype(jnp.float32), axis=0)
    grad_down_weight = jnp.einsum(
        "rf,rd->fd", hidden, grad_branch_two, preferred_element_type=jnp.float32
    )
    grad_hidden = jnp.einsum(
        "rd,fd->rf", grad_branch_two, down_weight, preferred_element_type=jnp.float32
    )
    unused_gelu, gelu_pull = jax.vjp(gelu_exact, hidden_pre)
    grad_pre = gelu_pull(grad_hidden)[0].astype(jnp.bfloat16)
    grad_up_bias = jnp.sum(grad_pre.astype(jnp.float32), axis=0)
    grad_up_weight = jnp.einsum(
        "rd,rf->df", normed_two, grad_pre, preferred_element_type=jnp.float32
    )
    grad_normed_two = jnp.einsum(
        "rf,df->rd", grad_pre, up_weight, preferred_element_type=jnp.float32
    )
    unused_norm, second_pull = jax.vjp(
        layer_norm, midway, feed_gain.astype(jnp.float32), feed_shift.astype(jnp.float32)
    )
    grad_midway, grad_feed_gain, grad_feed_shift = second_pull(grad_normed_two)
    grad_midway = grad_midway + upstream
    grad_attention_scale = jnp.sum(grad_midway * branch_one, axis=0)
    grad_branch_one = (grad_midway * attention_scale.astype(jnp.float32)).astype(jnp.bfloat16)
    grad_output_bias = jnp.sum(grad_branch_one.astype(jnp.float32), axis=0)
    grad_output_weight = jnp.einsum(
        "rc,rd->cd", attended, grad_branch_one, preferred_element_type=jnp.float32
    )
    grad_attended = jnp.einsum(
        "rd,cd->rc", grad_branch_one, output_weight, preferred_element_type=jnp.float32
    )
    grad_attended = grad_attended.astype(jnp.bfloat16).reshape(count, length, HEADS, HEAD)
    scores, query_part, key_part, value_part = attention_scores(triple, allowed, count, length)
    probabilities = jnp.exp(scores - log_total)
    grad_value = jnp.einsum(
        "bhqk,bqhd->bkhd",
        probabilities.astype(jnp.bfloat16),
        grad_attended,
        preferred_element_type=jnp.float32,
    )
    grad_probs = jnp.einsum(
        "bqhd,bkhd->bhqk", grad_attended, value_part, preferred_element_type=jnp.float32
    )
    grad_scores = probabilities * (
        grad_probs - jnp.sum(probabilities * grad_probs, axis=-1, keepdims=True)
    )
    grad_scores = grad_scores.astype(jnp.bfloat16)
    grad_query = jnp.einsum(
        "bhqk,bkhd->bqhd", grad_scores, key_part, preferred_element_type=jnp.float32
    ) * HEAD ** (-0.5)
    grad_key = jnp.einsum(
        "bhqk,bqhd->bkhd", grad_scores, query_part, preferred_element_type=jnp.float32
    ) * HEAD ** (-0.5)
    row_count = count * length
    grad_triple = jnp.concatenate(
        [
            grad_query.reshape(row_count, width),
            grad_key.reshape(row_count, width),
            grad_value.reshape(row_count, width),
        ],
        axis=1,
    ).astype(jnp.bfloat16)
    column_sums = jnp.sum(grad_triple.astype(jnp.float32), axis=0)
    grad_triple_bias = jnp.concatenate([column_sums[:width], column_sums[2 * width :]])
    grad_triple_weight = jnp.einsum(
        "rc,rd->cd", normed, grad_triple, preferred_element_type=jnp.float32
    )
    grad_normed = jnp.einsum(
        "rd,cd->rc", grad_triple, triple_weight, preferred_element_type=jnp.float32
    )
    unused_first, first_pull = jax.vjp(
        layer_norm,
        block_in,
        attention_gain.astype(jnp.float32),
        attention_shift.astype(jnp.float32),
    )
    grad_in, grad_attention_gain, grad_attention_shift = first_pull(grad_normed)
    grad_in = grad_in + grad_midway
    gradients_local = (
        grad_attention_gain,
        grad_attention_shift,
        grad_triple_weight,
        grad_triple_bias,
        grad_output_weight,
        grad_output_bias,
        grad_attention_scale,
        grad_feed_gain,
        grad_feed_shift,
        grad_up_weight,
        grad_up_bias,
        grad_down_weight,
        grad_down_bias,
        grad_feed_scale,
    )
    return (grad_in, gradients_local)


def local(
    block_io,
    segments,
    valid_tokens,
    attention_gain,
    attention_shift,
    triple_weight,
    triple_bias,
    output_weight,
    output_bias,
    attention_scale,
    feed_gain,
    feed_shift,
    up_weight,
    up_bias,
    down_weight,
    down_bias,
    feed_scale,
):
    params = tuple(
        (
            piece[0]
            for piece in (
                attention_gain,
                attention_shift,
                triple_weight,
                triple_bias,
                output_weight,
                output_bias,
                attention_scale,
                feed_gain,
                feed_shift,
                up_weight,
                up_bias,
                down_weight,
                down_bias,
                feed_scale,
            )
        )
    )
    section = lax.axis_index("section")
    leading = section == 0
    local_data = block_io[0]
    count = SPM
    length = local_data.shape[1]
    width = local_data.shape[2]
    steps_all = jnp.arange(MB + 1, dtype=jnp.int32)

    def forward_step(arrived, step):
        micro = jnp.clip(step - section, 0, MB - 1)
        fixed = jnp.minimum(step, MB - 1)
        own_input = micro_rows(local_data, fixed, count)
        section_input = jnp.where(leading, own_input, arrived)
        allowed = attention_mask(
            micro_rows(segments, micro, count), micro_rows(valid_tokens, micro, count)
        )
        result, stored = block_forward(section_input, params, allowed)
        sent = passed_along(result.astype(jnp.bfloat16).reshape(count, length, width), "section", 1)
        return (sent, (result, section_input))

    arrived_start = jnp.zeros((count, length, width), jnp.bfloat16)
    unused_arrived, (forward_results, stacked) = lax.scan(forward_step, arrived_start, steps_all)

    def backward_step(carry, step):
        totals, returned = carry
        micro = jnp.clip(MB - step - section, 0, MB - 1)
        position = jnp.clip(MB - step, 0, MB)
        active = jnp.where(leading, step >= 1, step < MB)
        allowed = attention_mask(
            micro_rows(segments, micro, count), micro_rows(valid_tokens, micro, count)
        )
        section_input = lax.dynamic_index_in_dim(stacked, position, 0, keepdims=False)
        unused_result, stored = block_forward(section_input, params, allowed)
        cotangent = micro_rows(local_data, micro, count)
        upstream = (
            jnp.where(leading, returned, cotangent)
            .astype(jnp.float32)
            .reshape(count * length, width)
        )
        upstream = jnp.where(active, upstream, 0.0)
        grad_in, gradients_local = block_backward(stored, upstream, params, allowed, count, length)
        totals = tuple((left + right for left, right in zip(totals, gradients_local)))
        returned = passed_along(
            grad_in.astype(jnp.bfloat16).reshape(count, length, width), "section", -1
        )
        return ((totals, returned), grad_in)

    totals_start = tuple((jnp.zeros(piece.shape, jnp.float32) for piece in params))
    returned_start = jnp.zeros((count, length, width), jnp.bfloat16)
    (totals, unused_returned), input_grads = lax.scan(
        backward_step, (totals_start, returned_start), steps_all
    )
    pieces_out = []
    for micro_index in range(MB):
        chosen = jnp.where(leading, input_grads[MB - micro_index], forward_results[micro_index + 1])
        pieces_out.append(chosen.reshape(count, length, width))
    block_ends = jnp.concatenate(pieces_out, axis=0)[None]
    expanded = [piece[None] for piece in totals]
    whole = lax.psum(
        (
            expanded[0],
            expanded[1],
            expanded[2],
            expanded[3],
            expanded[4],
            expanded[5],
            expanded[6],
            expanded[7],
            expanded[8],
            expanded[9],
            expanded[10],
            expanded[11],
            expanded[12],
            expanded[13],
        ),
        ("dp", "inner"),
    )
    return (
        block_ends,
        whole[0],
        whole[1],
        whole[2],
        whole[3],
        whole[4],
        whole[5],
        whole[6],
        whole[7],
        whole[8],
        whole[9],
        whole[10],
        whole[11],
        whole[12],
        whole[13],
    )


def solution(mesh):
    return jax.shard_map(
        local,
        mesh=mesh,
        in_specs=(
            P("section", ("dp", "inner"), None, None),
            P(("dp", "inner"), None),
            P(("dp", "inner"), None),
            P("section", None),
            P("section", None),
            P("section", None, None),
            P("section", None),
            P("section", None, None),
            P("section", None),
            P("section", None),
            P("section", None),
            P("section", None),
            P("section", None, None),
            P("section", None),
            P("section", None, None),
            P("section", None),
            P("section", None),
        ),
        out_specs=(
            P("section", ("dp", "inner"), None, None),
            P("section", None),
            P("section", None),
            P("section", None, None),
            P("section", None),
            P("section", None, None),
            P("section", None),
            P("section", None),
            P("section", None),
            P("section", None),
            P("section", None, None),
            P("section", None),
            P("section", None, None),
            P("section", None),
            P("section", None),
        ),
        check_vma=False,
    )
```

profile of v0, /device:TPU:0, one launch (start us, length us, event | category | flops | bytes accessed | tf_op | source)
XLA Modules:
  0.0 1041.3 jit_solution(15319867843428084041)
XLA Ops:
  21.0 174.0 %while.55 = (s32[]{:T(128)}, bf16[1,320,768]{2,1,0:T(8,128)(2,1)S(1)}, f32[3,320,768]{2,1,0:T(8,128)}, bf16[3,1,320,768]{3,2,1,0:T(8,128)(2,1)S(1)}, pred[]{:T(5...) while((s32[]{:T(128)}, ...), condition=%wide.region_7.8_spmd, body=%wide.region_0.7_spmd.sunk | while | flops 4926192640 | bytes 52212296 | solution.py:311
  38.3 5.9 fusion.263
  48.7 15.9 %bitcast_dynamic-update-slice_fusion.7 = (f32[3,320,768]{2,1,0:T(8,128)}, bf16[320,768]{1,0:T(8,128)(2,1)}) fusion(f32[3,320,768]{2,1,0:T(8,128)} %get-tuple-element.1195, s32[]{:T(128)} %get-tuple-element.1193, f32[320,768]{1,0:T(8,128)S(1)} %get-tuple-element.1078, f32[768]{0:T(1024)S(1)} %convert_element_type.478, ...), kind=kOutput, calls=%fused_computation.48.clone.1 | convolution fusion | flops 3086991360 | bytes 12911104 | tf_op jit(solution)/shard_map/while/body/eval_jaxpr/dot_general | solution.py:101
  64.6 4.9 collective-permute-start
  69.5 10.7 %collective-permute-done = bf16[1,320,768]{2,1,0:T(8,128)(2,1)S(1)} collective-permute-done((bf16[1,320,768]{2,1,0:T(8,128)(2,1)}, bf16[1,320,768]{2,1,0:T(8,128)(2,1)S(1)}, u32[]{:S(2)}, u32[]{:S(2)}) %collective-permute-start) | collective-permute-done | bytes 491552 | tf_op jit(solution)/shard_map/while/body/eval_jaxpr/ppermute | solution.py:15
  97.6 5.9 fusion.263
  108.0 15.9 %bitcast_dynamic-update-slice_fusion.7 = (f32[3,320,768]{2,1,0:T(8,128)}, bf16[320,768]{1,0:T(8,128)(2,1)}) fusion(f32[3,320,768]{2,1,0:T(8,128)} %get-tuple-element.1195, s32[]{:T(128)} %get-tuple-element.1193, f32[320,768]{1,0:T(8,128)S(1)} %get-tuple-element.1078, f32[768]{0:T(1024)S(1)} %convert_element_type.478, ...), kind=kOutput, calls=%fused_computation.48.clone.1 | convolution fusion | flops 3086991360 | bytes 12911104 | tf_op jit(solution)/shard_map/while/body/eval_jaxpr/dot_general | solution.py:101
  128.2 9.9 collective-permute-done
  155.4 5.9 fusion.263
  165.8 15.9 %bitcast_dynamic-update-slice_fusion.7 = (f32[3,320,768]{2,1,0:T(8,128)}, bf16[320,768]{1,0:T(8,128)(2,1)}) fusion(f32[3,320,768]{2,1,0:T(8,128)} %get-tuple-element.1195, s32[]{:T(128)} %get-tuple-element.1193, f32[320,768]{1,0:T(8,128)S(1)} %get-tuple-element.1078, f32[768]{0:T(1024)S(1)} %convert_element_type.478, ...), kind=kOutput, calls=%fused_computation.48.clone.1 | convolution fusion | flops 3086991360 | bytes 12911104 | tf_op jit(solution)/shard_map/while/body/eval_jaxpr/dot_general | solution.py:101
  186.0 9.0 collective-permute-done
  198.1 322.0 %while.56 = (s32[]{:T(128)}, f32[768]{0:T(1024)}, f32[768]{0:T(1024)}, f32[768,2304]{1,0:T(8,128)}, f32[1536]{0:T(1024)}, /*index=5*/f32[768,768]{1,0:T(8,128)},...) while((s32[]{:T(128)}, f32[768]{0:T(1024)}, ...), condition=%wide.region_30.31_spmd.clone, body=%wide.region_8.30_spmd.clone.sunk | while | flops 14693342208 | bytes 507242496 | solution.py:339
  225.4 13.1 %multiply_convert_fusion.6 = (bf16[320,3072]{1,0:T(8,128)(2,1)}, f32[320,3072]{1,0:T(8,128)S(1)}, f32[320,3072]{1,0:T(8,128)S(1)}) fusion(f32[3072]{0:T(1024)S(1)} %copy-done.58, bf16[768,3072]{1,0:T(8,128)(2,1)} %get-tuple-element.1368, f32[320,768]{1,0:T(8,128)S(1)} %get-tuple-element.1128, f32[768]{0:T(1024)S(1)} %convert_element_type.517, ...), kind=kOutput, calls=%fused_computation.120.clone.1 | convolution fusion | flops 1576058880 | bytes 15553024 | tf_op jit(solution)/shard_map/while/body/eval_jaxpr/dot_general | solution.py:97
  238.5 6.8 convert_reduce_fusion.14
  245.3 5.6 multiply_reduce_fusion.12
  277.9 6.7 select_add_fusion.23
  284.7 4.3 select_add_fusion.27
  293.0 5.6 select_add_fusion.29
  330.9 12.8 %multiply_convert_fusion.6 = (bf16[320,3072]{1,0:T(8,128)(2,1)}, f32[320,3072]{1,0:T(8,128)S(1)}, f32[320,3072]{1,0:T(8,128)S(1)}) fusion(f32[3072]{0:T(1024)S(1)} %copy-done.58, bf16[768,3072]{1,0:T(8,128)(2,1)} %get-tuple-element.1368, f32[320,768]{1,0:T(8,128)S(1)} %get-tuple-element.1128, f32[768]{0:T(1024)S(1)} %convert_element_type.517, ...), kind=kOutput, calls=%fused_computation.120.clone.1 | convolution fusion | flops 1576058880 | bytes 15553024 | tf_op jit(solution)/shard_map/while/body/eval_jaxpr/dot_general | solution.py:97
  343.6 6.9 convert_reduce_fusion.14
  350.5 5.6 multiply_reduce_fusion.12
  383.1 8.8 select_add_fusion.23
  400.3 5.8 select_add_fusion.29
  438.1 12.8 %multiply_convert_fusion.6 = (bf16[320,3072]{1,0:T(8,128)(2,1)}, f32[320,3072]{1,0:T(8,128)S(1)}, f32[320,3072]{1,0:T(8,128)S(1)}) fusion(f32[3072]{0:T(1024)S(1)} %copy-done.58, bf16[768,3072]{1,0:T(8,128)(2,1)} %get-tuple-element.1368, f32[320,768]{1,0:T(8,128)S(1)} %get-tuple-element.1128, f32[768]{0:T(1024)S(1)} %convert_element_type.517, ...), kind=kOutput, calls=%fused_computation.120.clone.1 | convolution fusion | flops 1576058880 | bytes 15553024 | tf_op jit(solution)/shard_map/while/body/eval_jaxpr/dot_general | solution.py:97
  450.9 6.9 convert_reduce_fusion.14
  457.9 5.6 multiply_reduce_fusion.12
  490.6 8.9 select_add_fusion.23
  507.9 5.5 select_add_fusion.29
  520.9 64.1 %all-reduce = (f32[1,768]{1,0:T(1,128)}, f32[1,768]{1,0:T(1,128)}, f32[1,1536]{1,0:T(1,128)}, f32[1,768]{1,0:T(1,128)}, f32[1,768]{1,0:T(1,128)}, /*index=5*/f32...) all-reduce(f32[1,768]{1,0:T(1,128)S(1)} %broadcast_in_dim.180, ...), channel_id=1, replica_groups=mesh['section'=2,'dp'=4,'inner'=4] {'dp','inner'}, use_global_device_ids=true, to_apply=%region_31.32 | all-reduce | flops 10752 | bytes 86016 | tf_op jit(solution)/shard_map/psum | solution.py:348
  588.2 426.2 %all-reduce.4.cloned.1.call-done = (f32[1,768,2304]{2,1,0:T(8,128)}, f32[1,768,768]{2,1,0:T(8,128)}, f32[1,768,3072]{2,1,0:T(8,128)}, f32[1,3072,768]{2,1,0:T(8,128)}) async-done(((f32[1,768,2304]{2,1,0:T(8,128)}, f32[1,768,768]{2,1,0:T(8,128)}, f32[1,768,3072]{2,1,0:T(8,128)}, f32[1,3072,768]{2,1,0:T(8,128)}), (f32[1,768,2304]{2,1,0:T(8,128)}, f32[1,768,768]{2,1,0:T(8,128)}, f32[1,768,3072]{2,1,0:T(8,128)}, ...) | async-done | bytes 28311568 | tf_op jit(solution)/shard_map/psum | solution.py:348
  1014.4 7.2 copy.151
  1024.2 4.8 copy.153
  (899 shorter events, 286.2 us)
Async XLA Ops:
  7.2 1007.2 %all-reduce.4.cloned.1.call-start = ((), (), s32[]{:S(2)}) async-start(), calls=%async_computation | async-start | bytes 56623104 | tf_op jit(solution)/shard_map/psum | solution.py:348
  64.6 15.6 %collective-permute-start = (bf16[1,320,768]{2,1,0:T(8,128)(2,1)}, bf16[1,320,768]{2,1,0:T(8,128)(2,1)S(1)}, u32[]{:S(2)}, u32[]{:S(2)}) collective-permute-start(bf16[1,320,768]{2,1,0:T(8,128)(2,1)} %bitcast.343), channel_id=1, source_target_pairs={{0,16},{1,17},{2,18},{3,19},{4,20},{5,21},{6,22},{7,23},{8,24},{9,... | collective-permute-start | bytes 1474568 | tf_op jit(solution)/shard_map/while/body/eval_jaxpr/ppermute | solution.py:15
  123.9 14.2 %collective-permute-start = (bf16[1,320,768]{2,1,0:T(8,128)(2,1)}, bf16[1,320,768]{2,1,0:T(8,128)(2,1)S(1)}, u32[]{:S(2)}, u32[]{:S(2)}) collective-permute-start(bf16[1,320,768]{2,1,0:T(8,128)(2,1)} %bitcast.343), channel_id=1, source_target_pairs={{0,16},{1,17},{2,18},{3,19},{4,20},{5,21},{6,22},{7,23},{8,24},{9,... | collective-permute-start | bytes 1474568 | tf_op jit(solution)/shard_map/while/body/eval_jaxpr/ppermute | solution.py:15
  181.7 13.3 %collective-permute-start = (bf16[1,320,768]{2,1,0:T(8,128)(2,1)}, bf16[1,320,768]{2,1,0:T(8,128)(2,1)S(1)}, u32[]{:S(2)}, u32[]{:S(2)}) collective-permute-start(bf16[1,320,768]{2,1,0:T(8,128)(2,1)} %bitcast.343), channel_id=1, source_target_pairs={{0,16},{1,17},{2,18},{3,19},{4,20},{5,21},{6,22},{7,23},{8,24},{9,... | collective-permute-start | bytes 1474568 | tf_op jit(solution)/shard_map/while/body/eval_jaxpr/ppermute | solution.py:15
  198.1 13.3 %copy-start.34 = (bf16[1536]{0:T(1024)(128)(2,1)}, bf16[1536]{0:T(1024)(128)(2,1)S(1)}, u32[]{:S(2)}) copy-start(bf16[1536]{0:T(1024)(128)(2,1)S(1)} %get-tuple-element.1359) | copy-start | bytes 9220 | tf_op jit(solution)/shard_map/while
  198.1 13.3 %copy-start.49 = (bf16[3072]{0:T(1024)(128)(2,1)}, bf16[3072]{0:T(1024)(128)(2,1)S(1)}, u32[]{:S(2)}) copy-start(bf16[3072]{0:T(1024)(128)(2,1)S(1)} %get-tuple-element.1369) | copy-start | bytes 18436 | tf_op jit(solution)/shard_map/while
  198.1 24.0 %copy-start.13 = (bf16[3,1,320,768]{3,2,1,0:T(8,128)(2,1)}, bf16[3,1,320,768]{3,2,1,0:T(8,128)(2,1)S(1)}, u32[]{:S(2)}) copy-start(bf16[3,1,320,768]{3,2,1,0:T(8,128)(2,1)S(1)} %get-tuple-element.1355) | copy-start | bytes 4423684 | tf_op jit(solution)/shard_map/while
  204.1 11.9 %copy-start.51 = (f32[320]{0:T(512)}, f32[320]{0:T(512)S(1)}, u32[]{:S(2)}) copy-start(f32[320]{0:T(512)S(1)} %fusion.296) | copy-start | bytes 3844 | tf_op jit(solution)/shard_map/while
  223.8 27.1 %copy-start.38 = (f32[320]{0:T(512)}, f32[320]{0:T(512)S(1)}, u32[]{:S(2)}) copy-start(f32[320]{0:T(512)S(1)} %broadcast_multiply_fusion.11) | copy-start | bytes 3844 | tf_op jit(solution)/shard_map/while
  224.1 26.9 %copy-start.47 = (f32[320]{0:T(512)}, f32[320]{0:T(512)S(1)}, u32[]{:S(2)}) copy-start(f32[320]{0:T(512)S(1)} %fusion.306) | copy-start | bytes 3844 | tf_op jit(solution)/shard_map/while
  225.4 13.1 %copy-start.40 = (f32[768]{0:T(1024)S(1)}, f32[768]{0:T(1024)}, u32[]{:S(2)}) copy-start(f32[768]{0:T(1024)} %convert_element_type.518) | copy-start | bytes 9220 | tf_op jit(solution)/shard_map/while
  272.5 27.7 %collective-permute-start.1 = (bf16[1,320,768]{2,1,0:T(8,128)(2,1)}, bf16[1,320,768]{2,1,0:T(8,128)(2,1)}, u32[]{:S(2)}, u32[]{:S(2)}) collective-permute-start(bf16[1,320,768]{2,1,0:T(8,128)(2,1)} %get-tuple-element.1164), channel_id=1, source_target_pairs={{16,0},{17,1},{18,2},{19,3},{20,4},{21,5},{22,6},{23,7},{24,8},{25... | collective-permute-start | bytes 1474568 | tf_op jit(solution)/shard_map/while/body/eval_jaxpr/ppermute | solution.py:15
  277.9 11.2 %slice-start.11 = ((s8[4718592]{0:T(1024)(128)(4,1)}), s8[4194304]{0:T(1024)(128)(4,1)S(1)}, s32[]{:S(2)}) async-start(s8[4718592]{0:T(1024)(128)(4,1)} %bitcast.340), calls=%async_computation.12 | async-start | bytes 8388608 | tf_op jit(solution)/shard_map/while
  303.5 13.3 %copy-start.34 = (bf16[1536]{0:T(1024)(128)(2,1)}, bf16[1536]{0:T(1024)(128)(2,1)S(1)}, u32[]{:S(2)}) copy-start(bf16[1536]{0:T(1024)(128)(2,1)S(1)} %get-tuple-element.1359) | copy-start | bytes 9220 | tf_op jit(solution)/shard_map/while
  303.5 13.3 %copy-start.49 = (bf16[3072]{0:T(1024)(128)(2,1)}, bf16[3072]{0:T(1024)(128)(2,1)S(1)}, u32[]{:S(2)}) copy-start(bf16[3072]{0:T(1024)(128)(2,1)S(1)} %get-tuple-element.1369) | copy-start | bytes 18436 | tf_op jit(solution)/shard_map/while
  303.6 24.0 %copy-start.13 = (bf16[3,1,320,768]{3,2,1,0:T(8,128)(2,1)}, bf16[3,1,320,768]{3,2,1,0:T(8,128)(2,1)S(1)}, u32[]{:S(2)}) copy-start(bf16[3,1,320,768]{3,2,1,0:T(8,128)(2,1)S(1)} %get-tuple-element.1355) | copy-start | bytes 4423684 | tf_op jit(solution)/shard_map/while
  309.6 11.9 %copy-start.51 = (f32[320]{0:T(512)}, f32[320]{0:T(512)S(1)}, u32[]{:S(2)}) copy-start(f32[320]{0:T(512)S(1)} %fusion.296) | copy-start | bytes 3844 | tf_op jit(solution)/shard_map/while
  329.3 26.8 %copy-start.38 = (f32[320]{0:T(512)}, f32[320]{0:T(512)S(1)}, u32[]{:S(2)}) copy-start(f32[320]{0:T(512)S(1)} %broadcast_multiply_fusion.11) | copy-start | bytes 3844 | tf_op jit(solution)/shard_map/while
  329.6 26.5 %copy-start.47 = (f32[320]{0:T(512)}, f32[320]{0:T(512)S(1)}, u32[]{:S(2)}) copy-start(f32[320]{0:T(512)S(1)} %fusion.306) | copy-start | bytes 3844 | tf_op jit(solution)/shard_map/while
  330.9 12.8 %copy-start.40 = (f32[768]{0:T(1024)S(1)}, f32[768]{0:T(1024)}, u32[]{:S(2)}) copy-start(f32[768]{0:T(1024)} %convert_element_type.518) | copy-start | bytes 9220 | tf_op jit(solution)/shard_map/while
  377.6 30.1 %collective-permute-start.1 = (bf16[1,320,768]{2,1,0:T(8,128)(2,1)}, bf16[1,320,768]{2,1,0:T(8,128)(2,1)}, u32[]{:S(2)}, u32[]{:S(2)}) collective-permute-start(bf16[1,320,768]{2,1,0:T(8,128)(2,1)} %get-tuple-element.1164), channel_id=1, source_target_pairs={{16,0},{17,1},{18,2},{19,3},{20,4},{21,5},{22,6},{23,7},{24,8},{25... | collective-permute-start | bytes 1474568 | tf_op jit(solution)/shard_map/while/body/eval_jaxpr/ppermute | solution.py:15
  383.1 13.3 %slice-start.11 = ((s8[4718592]{0:T(1024)(128)(4,1)}), s8[4194304]{0:T(1024)(128)(4,1)S(1)}, s32[]{:S(2)}) async-start(s8[4718592]{0:T(1024)(128)(4,1)} %bitcast.340), calls=%async_computation.12 | async-start | bytes 8388608 | tf_op jit(solution)/shard_map/while
  410.8 13.3 %copy-start.34 = (bf16[1536]{0:T(1024)(128)(2,1)}, bf16[1536]{0:T(1024)(128)(2,1)S(1)}, u32[]{:S(2)}) copy-start(bf16[1536]{0:T(1024)(128)(2,1)S(1)} %get-tuple-element.1359) | copy-start | bytes 9220 | tf_op jit(solution)/shard_map/while
  410.8 13.3 %copy-start.49 = (bf16[3072]{0:T(1024)(128)(2,1)}, bf16[3072]{0:T(1024)(128)(2,1)S(1)}, u32[]{:S(2)}) copy-start(bf16[3072]{0:T(1024)(128)(2,1)S(1)} %get-tuple-element.1369) | copy-start | bytes 18436 | tf_op jit(solution)/shard_map/while
  410.8 24.0 %copy-start.13 = (bf16[3,1,320,768]{3,2,1,0:T(8,128)(2,1)}, bf16[3,1,320,768]{3,2,1,0:T(8,128)(2,1)S(1)}, u32[]{:S(2)}) copy-start(bf16[3,1,320,768]{3,2,1,0:T(8,128)(2,1)S(1)} %get-tuple-element.1355) | copy-start | bytes 4423684 | tf_op jit(solution)/shard_map/while
  416.9 11.9 %copy-start.51 = (f32[320]{0:T(512)}, f32[320]{0:T(512)S(1)}, u32[]{:S(2)}) copy-start(f32[320]{0:T(512)S(1)} %fusion.296) | copy-start | bytes 3844 | tf_op jit(solution)/shard_map/while
  436.6 26.9 %copy-start.38 = (f32[320]{0:T(512)}, f32[320]{0:T(512)S(1)}, u32[]{:S(2)}) copy-start(f32[320]{0:T(512)S(1)} %broadcast_multiply_fusion.11) | copy-start | bytes 3844 | tf_op jit(solution)/shard_map/while
  436.9 26.6 %copy-start.47 = (f32[320]{0:T(512)}, f32[320]{0:T(512)S(1)}, u32[]{:S(2)}) copy-start(f32[320]{0:T(512)S(1)} %fusion.306) | copy-start | bytes 3844 | tf_op jit(solution)/shard_map/while
  438.1 12.8 %copy-start.40 = (f32[768]{0:T(1024)S(1)}, f32[768]{0:T(1024)}, u32[]{:S(2)}) copy-start(f32[768]{0:T(1024)} %convert_element_type.518) | copy-start | bytes 9220 | tf_op jit(solution)/shard_map/while
  485.0 30.0 %collective-permute-start.1 = (bf16[1,320,768]{2,1,0:T(8,128)(2,1)}, bf16[1,320,768]{2,1,0:T(8,128)(2,1)}, u32[]{:S(2)}, u32[]{:S(2)}) collective-permute-start(bf16[1,320,768]{2,1,0:T(8,128)(2,1)} %get-tuple-element.1164), channel_id=1, source_target_pairs={{16,0},{17,1},{18,2},{19,3},{20,4},{21,5},{22,6},{23,7},{24,8},{25... | collective-permute-start | bytes 1474568 | tf_op jit(solution)/shard_map/while/body/eval_jaxpr/ppermute | solution.py:15
  490.6 13.3 %slice-start.11 = ((s8[4718592]{0:T(1024)(128)(4,1)}), s8[4194304]{0:T(1024)(128)(4,1)S(1)}, s32[]{:S(2)}) async-start(s8[4718592]{0:T(1024)(128)(4,1)} %bitcast.340), calls=%async_computation.12 | async-start | bytes 8388608 | tf_op jit(solution)/shard_map/while
  520.2 64.8 %copy-start.32 = (f32[3,320,768]{2,1,0:T(8,128)S(1)}, f32[3,320,768]{2,1,0:T(8,128)}, u32[]{:S(2)}) copy-start(f32[3,320,768]{2,1,0:T(8,128)} %get-tuple-element.345) | copy-start | bytes 8847364
  (252 other events, 1142.7 us)
Sparse Core Ops, SparseCore 0:
  520.3 494.0 all-reduce.3
where the time goes:
time: 1060 us; the launch traced here: 1040 us
  waiting for transfers between devices  456 us (43%)
  matrix products  290 us (27%)
  other arithmetic  107 us (10%)
  local copies, waits for them, and re-layouts  75 us (7%)
  blocking collectives  64.1 us (6%)
  starting transfers between devices  18.3 us (2%)
  loops' own time  16.6 us (2%)
  between operations  14.7 us (1%)
    psum x1, waiting for transfers between devices, local(): lax.psum((expanded[0], expanded[1], expanded[2], expanded[3], expanded[4]...  426 us
    psum x1, blocking collectives, local(): lax.psum((expanded[0], expanded[1], expanded[2], expanded[3], expanded[4]...  64.1 us
    dot_general x6, matrix products, block_forward(): jnp.dot(hidden, down_weight, preferred_element_type=jnp.float32)  52.9 us
    dot_general x3, matrix products, block_forward(): jnp.dot(normed_two, up_weight, preferred_element_type=jnp.float32)  38.7 us
    ppermute x6, waiting for transfers between devices, passed_along(): lax.ppermute(value, axis, [(source, source + steps) for source in range(f...  29.6 us
    dot_general x3, matrix products, block_backward(): jnp.einsum('rc,rd->cd', normed, grad_triple, preferred_element_type=jnp.f...  24.5 us
  transfers between devices with their start and end apart: 7, of which 4 were waited for; matrix products, arithmetic and copies ran while one was open for 7% of the time, Pallas kernels for 0%

commit v1 on v0

v1 whole, which is shorter than its diff:
```python
import functools

import jax
import jax.numpy as jnp
from jax import lax
from jax.experimental import pallas as pl
from jax.experimental.pallas import tpu as pltpu
from jax.sharding import PartitionSpec as P

HEADS = 12
HEAD = 64
SCALE = HEAD ** (-0.5)
MESH = pl.DeviceIdType.MESH
F32 = jnp.float32
BF16 = jnp.bfloat16
CHUNK = 32
TILE = 256

FWD, DF, DU, DM, ATT, DX, WD, WU, WO, WT = range(10)

TAIL = 0.305
POLY = (
    0.12163973599672318,
    0.12246681749820709,
    0.10342079401016235,
    0.1210220605134964,
    -0.037977732717990875,
    0.18571804463863373,
    -0.15298904478549957,
    0.03669937700033188,
)

NT = (((1,), (1,)), ((), ()))


def nt_dot(left, right):
    return lax.dot_general(left, right, NT, preferred_element_type=F32)


def dot(left, right):
    return jnp.dot(left, right, preferred_element_type=F32)


def ds(start, size, multiple=None):
    if isinstance(start, int):
        return pl.ds(start, size)
    return pl.ds(pl.multiple_of(start, multiple or size), size)


def standardized(values):
    center = values - jnp.mean(values, axis=-1, keepdims=True)
    spread = jnp.mean(center * center, axis=-1, keepdims=True)
    inverse = lax.rsqrt(spread + 1e-06)
    return center * inverse, inverse


def norm_pull(grad, unit, inverse):
    first = jnp.mean(grad, axis=-1, keepdims=True)
    second = jnp.mean(grad * unit, axis=-1, keepdims=True)
    return inverse * (grad - first - unit * second)


def folded(values):
    rows, columns = values.shape
    return jnp.sum(values.reshape(rows // 8, 8, columns), axis=0)


def gelu_pair(values):
    size = jnp.abs(values)
    bell = jnp.exp(-0.5 * values * values)
    t = 1.0 / (1.0 + TAIL * size)
    acc = jnp.full_like(t, POLY[-1])
    for c in POLY[-2::-1]:
        acc = acc * t + c
    tail = acc * t * bell
    phi = jnp.where(values >= 0, 1.0 - tail, tail)
    return values * phi, phi + values * (bell * 0.3989422804014327)


def picked(table, slot):
    value = jnp.int32(table[0])
    for index in range(1, len(table)):
        if table[index] != table[index - 1]:
            value = jnp.where(slot >= index, jnp.int32(table[index]), value)
    return value


def schedules(count):
    parts = (DF, DU, DM, ATT, DX)
    first = [(FWD, m) for m in range(count)]
    for m in range(count - 1):
        first += [(part, m) for part in parts]
    last = count - 1
    first += [(DF, last), (WD, 0), (DU, last), (WU, 0), (DM, last), (WO, 0), (ATT, last), (WT, 0), (DX, last)]
    second = []
    for m in range(count):
        second += [(FWD, m)] + [(part, m) for part in parts]
    second += [(WD, 0), (WU, 0), (WO, 0), (WT, 0)]
    return first, second


def kernel(
    count, length, width, feed,
    data, key_code, query_code, ag, ash, tb, ob, asc, fg, fsh, ub, db, fsc, wt_h, wo_h, wu_h, wd_h,
    ends, gwt, gwo, gwu, gwd, vec,
    wt, wo, wu, wd, x, a, qkv, o, r, m, c, gp, h, f, g, df, dr, tmp, outb, bias, lse, prm, acc, acc_f, acc_t, lhs, stage,
    load_sem, out_sem, stage_sem, send_sem, recv_sem,
):
    section = lax.axis_index("section")
    leading = section == 0
    trailing = section == 1
    pairs = width // 128
    rows_all = count * length
    half = width // 2
    n_chunks = length // CHUNK

    weight_copies = [
        pltpu.make_async_copy(src, dst, load_sem.at[i])
        for i, (src, dst) in enumerate(((wt_h, wt), (wo_h, wo), (wu_h, wu), (wd_h, wd)))
    ]

    def rows_of(mb):
        return ds(mb * length, length, 64)

    def chunk_rows(mb, i):
        return ds(mb * length + i * CHUNK, CHUNK, CHUNK)

    def load_x(i):
        return pltpu.make_async_copy(data.at[i], x.at[pl.ds(i * length, length)], load_sem.at[4 + i])

    def load_g(i):
        return pltpu.make_async_copy(data.at[i], g.at[pl.ds(i * length, length)], load_sem.at[4 + i])

    def handed(mb):
        return pltpu.make_async_remote_copy(
            src_ref=dr.at[rows_of(mb)], dst_ref=x.at[rows_of(mb)],
            send_sem=send_sem.at[mb], recv_sem=recv_sem.at[mb],
            device_id={"section": 1 - section}, device_id_type=MESH,
        )

    def returned(mb):
        return pltpu.make_async_remote_copy(
            src_ref=g.at[rows_of(mb)], dst_ref=g.at[rows_of(mb)],
            send_sem=send_sem.at[mb], recv_sem=recv_sem.at[mb],
            device_id={"section": 1 - section}, device_id_type=MESH,
        )

    def out_copy(mb):
        return pltpu.make_async_copy(outb, ends.at[mb], out_sem)

    @pl.when(leading)
    def _():
        for i in range(count):
            load_x(i).start()

    for copy in weight_copies:
        copy.start()

    @pl.when(trailing)
    def _():
        for i in range(count):
            load_g(i).start()

    barrier = pltpu.get_barrier_semaphore()
    pl.semaphore_signal(barrier, inc=1, device_id={"section": 1 - section}, device_id_type=MESH)

    for row, ref in enumerate((ag, ash, ob, asc, fg, fsh, db, fsc)):
        prm[pl.ds(row, 1), pl.ds(0, width)] = ref[...].astype(F32)
    prm[pl.ds(8, 1), pl.ds(0, width)] = tb[:, pl.ds(0, width)].astype(F32)
    prm[pl.ds(8, 1), pl.ds(width, width)] = jnp.zeros((1, width), F32)
    prm[pl.ds(8, 1), pl.ds(2 * width, width)] = tb[:, pl.ds(width, width)].astype(F32)
    prm[pl.ds(9, 1), :] = ub[...].astype(F32)

    def param(row):
        return prm[pl.ds(row, 1), pl.ds(0, width)]

    acc[...] = jnp.zeros_like(acc)
    acc_f[...] = jnp.zeros_like(acc_f)
    acc_t[...] = jnp.zeros_like(acc_t)

    for i in range(count):
        same = key_code[i] == query_code[i]
        own = lax.broadcasted_iota(jnp.int32, (length, length), 0) == lax.broadcasted_iota(
            jnp.int32, (length, length), 1
        )
        bias[i] = jnp.where(same | own, 0.0, -1000000000.0)

    pl.semaphore_wait(barrier, 1)

    def forward(mb):
        rows = rows_of(mb)

        @pl.when(leading & (mb == 0))
        def _():
            for i in range(count):
                load_x(i).wait()

        @pl.when(trailing)
        def _():
            handed(mb).wait_recv()

        def norm_one(i, carry):
            rr = chunk_rows(mb, i)
            unit, unused = standardized(x[rr, :].astype(F32))
            a[rr, :] = (unit * param(0) + param(1)).astype(BF16)
            return carry

        lax.fori_loop(0, n_chunks, norm_one, 0)

        @pl.when(mb == 0)
        def _():
            weight_copies[0].wait()

        def triple(n, carry):
            cols = ds(n * TILE, TILE)
            qkv[rows, cols] = (dot(a[rows, :], wt[:, cols]) + prm[pl.ds(8, 1), cols]).astype(BF16)
            return carry

        lax.fori_loop(0, 3 * width // TILE, triple, 0)

        lane = lax.broadcasted_iota(jnp.int32, (length, 128), 1) < HEAD

        def attend(p, carry):
            q = qkv[rows, ds(p * 128, 128)]
            k = qkv[rows, ds(width + p * 128, 128)]
            v = qkv[rows, ds(2 * width + p * 128, 128)]
            zero = jnp.zeros_like(q)
            vt = v.T
            outs = []
            for hh in range(2):
                qm = jnp.where(lane, q, zero) if hh == 0 else jnp.where(lane, zero, q)
                s = nt_dot(k, qm) * SCALE + bias[mb]
                top = jnp.max(s, axis=0, keepdims=True)
                e = jnp.exp(s - top)
                total = jnp.sum(e, axis=0, keepdims=True)
                prob = (e * (1.0 / total)).astype(BF16)
                lse[mb, 2 * p + hh] = top + jnp.log(total)
                outs.append(dot(vt[hh * HEAD : (hh + 1) * HEAD], prob))
            o[rows, ds(p * 128, 128)] = jnp.concatenate(outs, axis=0).T.astype(BF16)
            return carry

        lax.fori_loop(0, pairs, attend, 0)

        @pl.when(mb == 0)
        def _():
            weight_copies[1].wait()

        def project(n, carry):
            cols = ds(n * TILE, TILE)
            res = dot(o[rows, :], wo[:, cols]) + prm[pl.ds(2, 1), cols]
            r[rows, cols] = res.astype(BF16)
            m[rows, cols] = x[rows, cols].astype(F32) + prm[pl.ds(3, 1), cols] * res
            return carry

        lax.fori_loop(0, width // TILE, project, 0)

        def norm_two(i, carry):
            rr = chunk_rows(mb, i)
            unit, unused = standardized(m[rr, :])
            c[rr, :] = (unit * param(4) + param(5)).astype(BF16)
            return carry

        lax.fori_loop(0, n_chunks, norm_two, 0)

        @pl.when(mb == 0)
        def _():
            weight_copies[2].wait()

        def up(n, carry):
            cols = ds(n * TILE, TILE)
            u = dot(c[rows, :], wu[:, cols]) + prm[pl.ds(9, 1), cols]
            value, slope = gelu_pair(u)
            h[rows, cols] = value.astype(BF16)
            gp[rows, cols] = slope.astype(BF16)
            return carry

        lax.fori_loop(0, feed // TILE, up, 0)

        @pl.when(mb == 0)
        def _():
            weight_copies[3].wait()

        @pl.when(trailing & (mb > 0))
        def _():
            out_copy(mb - 1).wait()

        def down(n, carry):
            cols = ds(n * TILE, TILE)
            res = dot(h[rows, :], wd[:, cols]) + prm[pl.ds(6, 1), cols]
            f[rows, cols] = res.astype(BF16)
            y = m[rows, cols] + prm[pl.ds(7, 1), cols] * res
            outb[:, cols] = y
            dr[rows, cols] = y.astype(BF16)
            return carry

        lax.fori_loop(0, width // TILE, down, 0)

        @pl.when(leading)
        def _():
            handed(mb).start()

        @pl.when(trailing)
        def _():
            out_copy(mb).start()

    def add_acc(row, values):
        acc[row] += folded(values)

    def grad_f(mb):
        @pl.when(leading)
        def _():
            returned(mb).wait_recv()

        @pl.when(trailing & (mb == 0))
        def _():
            for i in range(count):
                load_g(i).wait()

        def body(i, carry):
            rr = chunk_rows(mb, i)
            up_grad = g[rr, :].astype(F32)
            add_acc(7, up_grad * f[rr, :].astype(F32))
            value = (up_grad * param(7)).astype(BF16)
            df[rr, :] = value
            add_acc(6, value.astype(F32))
            return carry

        lax.fori_loop(0, n_chunks, body, 0)

    def grad_u(mb):
        rows = rows_of(mb)

        def body(n, carry):
            cols = ds(n * TILE, TILE)
            value = (nt_dot(df[rows, :], wd[cols, :]) * gp[rows, cols].astype(F32)).astype(BF16)
            gp[rows, cols] = value
            acc_f[:, cols] += folded(value.astype(F32))
            return carry

        lax.fori_loop(0, feed // TILE, body, 0)

    def grad_m(mb):
        rows = rows_of(mb)

        @pl.when(leading & (mb == 0))
        def _():
            for i in range(count):
                handed(i).wait_send()

        def first(n, carry):
            cols = ds(n * TILE, TILE)
            tmp[:, cols] = nt_dot(gp[rows, :], wu[cols, :])
            return carry

        lax.fori_loop(0, width // TILE, first, 0)

        def body(i, carry):
            rr = chunk_rows(mb, i)
            grad = tmp[ds(i * CHUNK, CHUNK), :]
            unit, inverse = standardized(m[rr, :])
            add_acc(4, grad * unit)
            add_acc(5, grad)
            total = g[rr, :].astype(F32) + norm_pull(grad * param(4), unit, inverse)
            m[rr, :] = total
            add_acc(3, total * r[rr, :].astype(F32))
            value = (total * param(3)).astype(BF16)
            dr[rr, :] = value
            add_acc(2, value.astype(F32))
            return carry

        lax.fori_loop(0, n_chunks, body, 0)

        def second(n, carry):
            cols = ds(n * TILE, TILE)
            g[rows, cols] = nt_dot(dr[rows, :], wo[cols, :]).astype(BF16)
            return carry

        lax.fori_loop(0, width // TILE, second, 0)

    def grad_attend(mb):
        rows = rows_of(mb)
        lane = lax.broadcasted_iota(jnp.int32, (length, 128), 1) < HEAD

        def body(p, carry):
            qc, kc, vc = (ds(part * width + p * 128, 128) for part in range(3))
            q, k, v, do = qkv[rows, qc], qkv[rows, kc], qkv[rows, vc], g[rows, qc]
            zero = jnp.zeros_like(q)
            kt = k.T
            dq = []
            dk = jnp.zeros((length, 128), F32)
            dv = jnp.zeros((length, 128), F32)
            for hh in range(2):
                qm = jnp.where(lane, q, zero) if hh == 0 else jnp.where(lane, zero, q)
                dom = jnp.where(lane, do, zero) if hh == 0 else jnp.where(lane, zero, do)
                s = nt_dot(k, qm) * SCALE + bias[mb]
                prob = jnp.exp(s - lse[mb, 2 * p + hh])
                dv = dv + dot(prob.astype(BF16), dom)
                dp = nt_dot(v, dom)
                inner = jnp.sum(prob * dp, axis=0, keepdims=True)
                grad = (prob * (dp - inner)).astype(BF16)
                dk = dk + dot(grad, qm)
                dq.append(dot(kt[hh * HEAD : (hh + 1) * HEAD], grad))
            dq = (jnp.concatenate(dq, axis=0).T * SCALE).astype(BF16)
            dk = (dk * SCALE).astype(BF16)
            dv = dv.astype(BF16)
            qkv[rows, qc] = dq
            qkv[rows, kc] = dk
            qkv[rows, vc] = dv
            acc_t[:, qc] += folded(dq.astype(F32))
            acc_t[:, vc] += folded(dv.astype(F32))
            return carry

        lax.fori_loop(0, pairs, body, 0)

    def grad_x(mb):
        rows = rows_of(mb)

        def first(n, carry):
            cols = ds(n * TILE, TILE)
            tmp[:, cols] = nt_dot(qkv[rows, :], wt[cols, :])
            return carry

        lax.fori_loop(0, width // TILE, first, 0)

        @pl.when(leading & (mb > 0))
        def _():
            out_copy(mb - 1).wait()

        @pl.when(trailing & (mb == count - 1))
        def _():
            out_copy(mb).wait()

        def body(i, carry):
            rr = chunk_rows(mb, i)
            grad = tmp[ds(i * CHUNK, CHUNK), :]
            unit, inverse = standardized(x[rr, :].astype(F32))
            add_acc(0, grad * unit)
            add_acc(1, grad)
            total = m[rr, :] + norm_pull(grad * param(0), unit, inverse)

            @pl.when(leading)
            def _():
                outb[ds(i * CHUNK, CHUNK), :] = total

            g[rr, :] = total.astype(BF16)
            return carry

        lax.fori_loop(0, n_chunks, body, 0)

        @pl.when(leading)
        def _():
            out_copy(mb).start()

        @pl.when(trailing)
        def _():
            returned(mb).start()

    def weight_grad(left, right, blocks, target, along_rows):
        def body(i, carry):
            block, part = i // 2, i % 2
            if along_rows:
                lhs[...] = left[:, ds(i * half, half)].T
                r0, c0, rc0 = i * half, 0, 0
            else:
                lhs[...] = left[:, ds(part * half, half)].T
                r0, c0, rc0 = part * half, block * width, block * width

            def tile(n, inner):
                cols = ds(n * TILE, TILE)
                stage[:, cols] = dot(lhs[...], right[:, ds(rc0 + n * TILE, TILE)]).astype(BF16)
                return inner

            lax.fori_loop(0, width // TILE, tile, 0)
            copy = pltpu.make_async_copy(
                stage, target.at[ds(r0, half), ds(c0, width, 128)], stage_sem
            )
            copy.start()
            copy.wait()
            return carry

        lax.fori_loop(0, 2 * blocks, body, 0)

    def slot_body(slot, carry):
        one, two = schedules(count)
        phase = jnp.where(leading, picked([e[0] for e in one], slot), picked([e[0] for e in two], slot))
        mb = jnp.where(leading, picked([e[1] for e in one], slot), picked([e[1] for e in two], slot))
        for which, act in ((FWD, forward), (DF, grad_f), (DU, grad_u), (DM, grad_m), (ATT, grad_attend), (DX, grad_x)):
            pl.when(phase == which)(functools.partial(act, mb))
        pl.when(phase == WD)(lambda: weight_grad(h, df, feed // width, gwd, True))
        pl.when(phase == WU)(lambda: weight_grad(c, gp, feed // width, gwu, False))
        pl.when(phase == WO)(lambda: weight_grad(o, dr, 1, gwo, False))
        pl.when(phase == WT)(lambda: weight_grad(a, qkv, 3, gwt, False))
        return carry

    lax.fori_loop(0, len(schedules(count)[0]), slot_body, 0)

    for row in range(8):
        vec[pl.ds(row, 1), pl.ds(0, width)] = jnp.sum(acc[row], axis=0, keepdims=True)
    vec[pl.ds(8, 1), pl.ds(0, 3 * width)] = jnp.sum(acc_t[...], axis=0, keepdims=True)
    vec[pl.ds(9, 1), :] = jnp.sum(acc_f[...], axis=0, keepdims=True)

    @pl.when(leading)
    def _():
        out_copy(count - 1).wait()

    @pl.when(trailing)
    def _():
        for i in range(count):
            returned(i).wait_send()


def local(
    block_io, segments, valid_tokens, attention_gain, attention_shift, triple_weight, triple_bias,
    output_weight, output_bias, attention_scale, feed_gain, feed_shift, up_weight, up_bias,
    down_weight, down_bias, feed_scale,
):
    count, length, width = block_io.shape[1:]
    feed = up_weight.shape[2]
    rows = count * length
    key_code = jnp.where(valid_tokens == 1, segments, -1)[:, :, None]
    query_code = segments[:, None, :]
    any_spec = pl.BlockSpec(memory_space=pl.ANY)
    vmem = pl.BlockSpec(memory_space=pltpu.VMEM)
    outs = pl.pallas_call(
        functools.partial(kernel, count, length, width, feed),
        out_shape=(
            jax.ShapeDtypeStruct((count, length, width), F32),
            jax.ShapeDtypeStruct((width, 3 * width), BF16),
            jax.ShapeDtypeStruct((width, width), BF16),
            jax.ShapeDtypeStruct((width, feed), BF16),
            jax.ShapeDtypeStruct((feed, width), BF16),
            jax.ShapeDtypeStruct((16, feed), F32),
        ),
        in_specs=[any_spec] + [vmem] * 12 + [any_spec] * 4,
        out_specs=(any_spec,) * 5 + (vmem,),
        scratch_shapes=[
            pltpu.VMEM((width, 3 * width), BF16),
            pltpu.VMEM((width, width), BF16),
            pltpu.VMEM((width, feed), BF16),
            pltpu.VMEM((feed, width), BF16),
            pltpu.VMEM((rows, width), BF16),
            pltpu.VMEM((rows, width), BF16),
            pltpu.VMEM((rows, 3 * width), BF16),
            pltpu.VMEM((rows, width), BF16),
            pltpu.VMEM((rows, width), BF16),
            pltpu.VMEM((rows, width), F32),
            pltpu.VMEM((rows, width), BF16),
            pltpu.VMEM((rows, feed), BF16),
            pltpu.VMEM((rows, feed), BF16),
            pltpu.VMEM((rows, width), BF16),
            pltpu.VMEM((rows, width), BF16),
            pltpu.VMEM((rows, width), BF16),
            pltpu.VMEM((rows, width), BF16),
            pltpu.VMEM((length, width), F32),
            pltpu.VMEM((length, width), F32),
            pltpu.VMEM((count, length, length), F32),
            pltpu.VMEM((count, HEADS, 1, length), F32),
            pltpu.VMEM((16, feed), F32),
            pltpu.VMEM((8, 8, width), F32),
            pltpu.VMEM((8, feed), F32),
            pltpu.VMEM((8, 3 * width), F32),
            pltpu.VMEM((width // 2, rows), BF16),
            pltpu.VMEM((width // 2, width), BF16),
            pltpu.SemaphoreType.DMA((4 + count,)),
            pltpu.SemaphoreType.DMA,
            pltpu.SemaphoreType.DMA,
            pltpu.SemaphoreType.DMA((count,)),
            pltpu.SemaphoreType.DMA((count,)),
        ],
        compiler_params=pltpu.CompilerParams(
            collective_id=0, has_side_effects=True, vmem_limit_bytes=62 << 20
        ),
    )(
        block_io[0], key_code, query_code, attention_gain, attention_shift, triple_bias, output_bias,
        attention_scale, feed_gain, feed_shift, up_bias, down_bias, feed_scale,
        triple_weight[0], output_weight[0], up_weight[0], down_weight[0],
    )
    ends, gwt, gwo, gwu, gwd, vec = outs
    gwt, gwo, gwu, gwd, vec = lax.psum((gwt, gwo, gwu, gwd, vec), ("dp", "inner"))

    def row(index):
        return vec[index : index + 1, :width]

    return (
        ends[None],
        row(0),
        row(1),
        gwt.astype(F32)[None],
        jnp.concatenate([vec[8:9, :width], vec[8:9, 2 * width : 3 * width]], axis=1),
        gwo.astype(F32)[None],
        row(2),
        row(3),
        row(4),
        row(5),
        gwu.astype(F32)[None],
        vec[9:10, :],
        gwd.astype(F32)[None],
        row(6),
        row(7),
    )


def solution(mesh):
    split = ("dp", "inner")
    matrix = P("section", None, None)
    vector = P("section", None)
    return jax.shard_map(
        local,
        mesh=mesh,
        in_specs=(
            P("section", split, None, None), P(split, None), P(split, None),
            vector, vector, matrix, vector, matrix, vector, vector, vector, vector,
            matrix, vector, matrix, vector, vector,
        ),
        out_specs=(
            P("section", split, None, None),
            vector, vector, matrix, vector, matrix, vector, vector, vector, vector,
            matrix, vector, matrix, vector, vector,
        ),
        check_vma=False,
    )
```

time: 1060 us -> 601 us (0.57); the launches traced: 1040 us -> 600 us
  matrix products: 290 us -> 0 us
  Pallas kernels: 0 us -> 213 us
  waiting for transfers between devices: 456 us -> 348 us
  other arithmetic: 107 us -> 18.4 us
  local copies, waits for them, and re-layouts: 75 us -> 6.77 us
  blocking collectives: 64.1 us -> 0 us
  starting transfers between devices: 18.3 us -> 0.08 us
  loops' own time: 16.6 us -> 0 us
    dot_general x66 -> x0, matrix products: 273 us -> none  [the longest x6 52.9 us: block_forward(): jnp.dot(hidden, down_weight, preferred_element_type=jnp.float32)]
    pallas_call x0 -> x1, Pallas kernels: none -> 213 us  [local(): pl.pallas_call(functools.partial(kernel, count, length, width, feed), out...]
    psum x1 -> x2, waiting for transfers between devices: 426 us -> 348 us  [local(): lax.psum((gwt, gwo, gwu, gwd, vec), ('dp', 'inner'))]
    psum x1 -> x0, blocking collectives: 64.1 us -> none  [local(): lax.psum((expanded[0], expanded[1], expanded[2], expanded[3], expanded[4]...]
    convert_element_type x57 -> x0, other arithmetic: 43.8 us -> none  [the longest x6 5.88 us: block_forward(): output_bias.astype(jnp.float32)]
    ppermute x6 -> x0, waiting for transfers between devices: 29.6 us -> none  [passed_along(): lax.ppermute(value, axis, [(source, source + steps) for source in range(f...]
    reduce_sum x36 -> x0, other arithmetic: 24.4 us -> none  [the longest x12 6.61 us: layer_norm(): center = values - jnp.mean(values, axis=-1, keepdims=True)]
    while x525 -> x0, local copies, waits for them, and re-layouts: 20 us -> none
  transfers between devices with their start and end apart: 7 -> 2, of which waited for: 4 -> 2; matrix products, arithmetic and copies ran while one was open for 7% -> 1% of each run, Pallas kernels for 0% -> 0%
where the time goes in v1:
time: 601 us; the launch traced here: 600 us
  waiting for transfers between devices  348 us (58%)
  Pallas kernels  213 us (35%)
  other arithmetic  18.4 us (3%)
  between operations  14.1 us (2%)
  local copies, waits for them, and re-layouts  6.77 us (1%)
    psum x2, waiting for transfers between devices, local(): lax.psum((gwt, gwo, gwu, gwd, vec), ('dp', 'inner'))  348 us
    pallas_call x1, Pallas kernels, local(): pl.pallas_call(functools.partial(kernel, count, length, width, feed), out...  213 us
  transfers between devices with their start and end apart: 2, of which 2 were waited for; matrix products, arithmetic and copies ran while one was open for 1% of the time, Pallas kernels for 0%

profile of v1, /device:TPU:0, one launch (start us, length us, event | category | flops | bytes accessed | tf_op | source)
XLA Modules:
  0.0 600.5 jit_solution(16278610141297211711)
XLA Ops:
  7.2 0.0 all-reduce.4.cloned.1.call-start
  7.2 1.3 broadcast_in_dim.39.query_code
  8.5 0.7 fusion
  9.2 0.9 copy.32.key_code
  10.1 212.9 %shard_map.280 = (f32[2,320,768]{2,1,0:T(8,128)}, bf16[768,2304]{1,0:T(8,128)(2,1)}, bf16[768,768]{1,0:T(8,128)(2,1)}, bf16[768,3072]{1,0:T(8,128)(2,1)}, bf16[3072,768]{1,0:T(8,128)(2,1)}, /*index=5*/f32[16,3072]{1,0:T(8,128)}) custom-call(bf16[2,320,768]{2,1,0:T(8,128)(2,1)} %bitcast.21, s32[2,320,1]{2,1,0:T(8,128)} %copy.32.key_code, ...), custom_call_target="tpu_custom_call" | custom-call | tf_op jit(solution)/shard_map/pallas_call | solution.py:524
  223.0 0.0 all-reduce.4.cloned.1.call-update
  223.0 0.0 all-reduce.6.cloned.1.call-start
  223.1 0.7 all-reduce.6.cloned.1.call-update
  223.8 89.3 %all-reduce.4.cloned.1.call-done = f32[16,3072]{1,0:T(8,128)} async-done(((f32[16,3072]{1,0:T(8,128)}), f32[16,3072]{1,0:T(8,128)}) %all-reduce.4.cloned.1.call-update) | async-done | bytes 196624 | tf_op jit(solution)/shard_map/psum | solution.py:579
  313.1 1.5 slice.52
  314.6 1.8 fusion.1
  316.4 0.6 pad_maximum_fusion
  317.0 258.3 %all-reduce.6.cloned.1.call-done = (bf16[1,768,2304]{2,1,0:T(8,128)(2,1)}, bf16[1,768,768]{2,1,0:T(8,128)(2,1)}, bf16[1,768,3072]{2,1,0:T(8,128)(2,1)}, bf16[1,3072,768]{2,1,0:T(8,128)(2,1)}) async-done(((bf16[1,768,2304]{2,1,0:T(8,128)(2,1)}, bf16[1,768,768]{2,1,0:T(8,128)(2,1)}, bf16[1,768,3072]{2,1,0:T(8,128)(2,1)}, bf16[1,3072,768]{2,1,0:T(8,128)(2,1)}), (bf16[1,768,2304]{2,1,0:T(8,128)(2,1)}, ...) | async-done | bytes 14155792 | tf_op jit(solution)/shard_map/psum | solution.py:579
  575.3 0.0 copy-start
  575.3 7.5 %broadcast_in_dim.46 = f32[1,768,3072]{2,1,0:T(8,128)} convert(bf16[1,768,3072]{2,1,0:T(8,128)(2,1)} %get-tuple-element.29) | non-fusion elementwise | flops 2359296 | bytes 14155776 | tf_op jit(solution)/shard_map/broadcast_in_dim | solution.py:595
  582.8 0.0 copy-done
  582.8 0.0 copy-start.1
  582.8 4.5 broadcast_in_dim.48
  587.3 0.0 copy-done.1
  587.3 0.0 copy-start.3
  587.3 0.0 copy-start.2
  587.3 3.5 broadcast_in_dim.42
  590.8 0.0 copy-done.3
  590.8 1.6 broadcast_in_dim.44
  592.4 0.0 copy-done.2
  592.4 1.3 copy.39
Async XLA Ops:
  7.2 305.9 %all-reduce.4.cloned.1.call-start = ((), (), s32[]{:S(2)}) async-start(), calls=%async_computation | async-start | bytes 393216 | tf_op jit(solution)/shard_map/psum | solution.py:579
  223.0 352.3 %all-reduce.6.cloned.1.call-start = ((), (), s32[]{:S(2)}) async-start(), calls=%async_computation.1 | async-start | bytes 28311552 | tf_op jit(solution)/shard_map/psum | solution.py:579
  575.3 7.5 %copy-start = (bf16[1,3072,768]{2,1,0:T(8,128)(2,1)S(1)}, bf16[1,3072,768]{2,1,0:T(8,128)(2,1)}, u32[]{:S(2)}) copy-start(bf16[1,3072,768]{2,1,0:T(8,128)(2,1)} %get-tuple-element.30) | copy-start | bytes 14155780
  582.8 4.5 copy-start.1
  587.3 3.5 copy-start.3
  587.3 5.1 copy-start.2
Sparse Core Ops, SparseCore 0:
  223.1 89.9 all-reduce.3
  317.6 257.6 all-reduce.5

commit v2 on v1

--- a/solution.py
+++ b/solution.py
@@ -16,7 +16,7 @@
 CHUNK = 32
 TILE = 256
 
-FWD, DF, DU, DM, ATT, DX, WD, WU, WO, WT = range(10)
+FWD, DF, DU, DM, ATT, DX, WD, WU, WT = range(9)
 
 TAIL = 0.305
 POLY = (
@@ -91,20 +91,23 @@
     for m in range(count - 1):
         first += [(part, m) for part in parts]
     last = count - 1
-    first += [(DF, last), (WD, 0), (DU, last), (WU, 0), (DM, last), (WO, 0), (ATT, last), (WT, 0), (DX, last)]
+    first += [(DF, last), (WD, 0), (DU, last), (WU, 0), (DM, last), (ATT, last), (WT, 0), (DX, last)]
     second = []
     for m in range(count):
         second += [(FWD, m)] + [(part, m) for part in parts]
-    second += [(WD, 0), (WU, 0), (WO, 0), (WT, 0)]
+    second += [(WD, 0), (WU, 0), (WT, 0)]
     return first, second
 
 
 def kernel(
-    count, length, width, feed,
+    count, length, width, feed, lines, depth, group,
     data, key_code, query_code, ag, ash, tb, ob, asc, fg, fsh, ub, db, fsc, wt_h, wo_h, wu_h, wd_h,
-    ends, gwt, gwo, gwu, gwd, vec,
-    wt, wo, wu, wd, x, a, qkv, o, r, m, c, gp, h, f, g, df, dr, tmp, outb, bias, lse, prm, acc, acc_f, acc_t, lhs, stage,
-    load_sem, out_sem, stage_sem, send_sem, recv_sem,
+    ends, blocks, vec,
+    wt, wo, wu, wd, x, a, qkv, o, r, m, c, gp, h, f, g, df, dr, tmp, outb, bias, lse, prm, acc, acc_f, acc_t, lhs,
+    part, twin_part, arrived, vpart, vtwin, varrived,
+    load_sem, out_sem, send_sem, recv_sem, stage_send, twin_recv,
+    sum_send, sum_recv, all_send, all_recv, pair_send, pair_recv, own_sem,
+    vsum_send, vsum_recv, vall_send, vall_recv, vpair_send, vpair_recv,
 ):
     section = lax.axis_index("section")
     leading = section == 0
@@ -161,8 +164,22 @@
         for i in range(count):
             load_g(i).start()
 
+    dp, z = lax.axis_index("dp"), lax.axis_index("inner")
+    core, y = dp % 2, dp // 2
+    ring = lines * depth
+    place = y * depth + jnp.where(y % 2 == 0, z, depth - 1 - z)
+
+    def ring_device(index):
+        index = lax.rem(index + ring, ring)
+        row, along = index // depth, index % depth
+        return {"dp": row * 2 + core, "inner": jnp.where(row % 2 == 0, along, depth - 1 - along)}
+
+    neighbours = (ring_device(place + 1), ring_device(place - 1))
+    sibling = {"dp": y * 2 + 1 - core}
+
     barrier = pltpu.get_barrier_semaphore()
-    pl.semaphore_signal(barrier, inc=1, device_id={"section": 1 - section}, device_id_type=MESH)
+    for device in ({"section": 1 - section}, sibling) + neighbours:
+        pl.semaphore_signal(barrier, inc=1, device_id=device, device_id_type=MESH)
 
     for row, ref in enumerate((ag, ash, ob, asc, fg, fsh, db, fsc)):
         prm[pl.ds(row, 1), pl.ds(0, width)] = ref[...].astype(F32)
@@ -185,42 +202,33 @@
         )
         bias[i] = jnp.where(same | own, 0.0, -1000000000.0)
 
-    pl.semaphore_wait(barrier, 1)
-
-    def forward(mb):
-        rows = rows_of(mb)
-
-        @pl.when(leading & (mb == 0))
-        def _():
-            for i in range(count):
-                load_x(i).wait()
-
-        @pl.when(trailing)
-        def _():
-            handed(mb).wait_recv()
-
-        def norm_one(i, carry):
+    pl.semaphore_wait(barrier, 4)
+
+    lane = lax.broadcasted_iota(jnp.int32, (length, 128), 1) < HEAD
+
+    def norm_one(mb):
+        def body(i, carry):
             rr = chunk_rows(mb, i)
             unit, unused = standardized(x[rr, :].astype(F32))
             a[rr, :] = (unit * param(0) + param(1)).astype(BF16)
             return carry
 
-        lax.fori_loop(0, n_chunks, norm_one, 0)
-
-        @pl.when(mb == 0)
-        def _():
-            weight_copies[0].wait()
-
-        def triple(n, carry):
+        lax.fori_loop(0, n_chunks, body, 0)
+
+    def triple(mb):
+        rows = rows_of(mb)
+
+        def body(n, carry):
             cols = ds(n * TILE, TILE)
             qkv[rows, cols] = (dot(a[rows, :], wt[:, cols]) + prm[pl.ds(8, 1), cols]).astype(BF16)
             return carry
 
-        lax.fori_loop(0, 3 * width // TILE, triple, 0)
-
-        lane = lax.broadcasted_iota(jnp.int32, (length, 128), 1) < HEAD
-
-        def attend(p, carry):
+        lax.fori_loop(0, 3 * width // TILE, body, 0)
+
+    def attend(mb):
+        rows = rows_of(mb)
+
+        def body(p, carry):
             q = qkv[rows, ds(p * 128, 128)]
             k = qkv[rows, ds(width + p * 128, 128)]
             v = qkv[rows, ds(2 * width + p * 128, 128)]
@@ -239,34 +247,33 @@
             o[rows, ds(p * 128, 128)] = jnp.concatenate(outs, axis=0).T.astype(BF16)
             return carry
 
-        lax.fori_loop(0, pairs, attend, 0)
-
-        @pl.when(mb == 0)
-        def _():
-            weight_copies[1].wait()
-
-        def project(n, carry):
+        lax.fori_loop(0, pairs, body, 0)
+
+    def project(mb):
+        rows = rows_of(mb)
+
+        def body(n, carry):
             cols = ds(n * TILE, TILE)
             res = dot(o[rows, :], wo[:, cols]) + prm[pl.ds(2, 1), cols]
             r[rows, cols] = res.astype(BF16)
             m[rows, cols] = x[rows, cols].astype(F32) + prm[pl.ds(3, 1), cols] * res
             return carry
 
-        lax.fori_loop(0, width // TILE, project, 0)
-
-        def norm_two(i, carry):
+        lax.fori_loop(0, width // TILE, body, 0)
+
+    def norm_two(mb):
+        def body(i, carry):
             rr = chunk_rows(mb, i)
             unit, unused = standardized(m[rr, :])
             c[rr, :] = (unit * param(4) + param(5)).astype(BF16)
             return carry
 
-        lax.fori_loop(0, n_chunks, norm_two, 0)
-
-        @pl.when(mb == 0)
-        def _():
-            weight_copies[2].wait()
-
-        def up(n, carry):
+        lax.fori_loop(0, n_chunks, body, 0)
+
+    def up(mb):
+        rows = rows_of(mb)
+
+        def body(n, carry):
             cols = ds(n * TILE, TILE)
             u = dot(c[rows, :], wu[:, cols]) + prm[pl.ds(9, 1), cols]
             value, slope = gelu_pair(u)
@@ -274,17 +281,12 @@
             gp[rows, cols] = slope.astype(BF16)
             return carry
 
-        lax.fori_loop(0, feed // TILE, up, 0)
-
-        @pl.when(mb == 0)
-        def _():
-            weight_copies[3].wait()
-
-        @pl.when(trailing & (mb > 0))
-        def _():
-            out_copy(mb - 1).wait()
-
-        def down(n, carry):
+        lax.fori_loop(0, feed // TILE, body, 0)
+
+    def down(mb):
+        rows = rows_of(mb)
+
+        def body(n, carry):
             cols = ds(n * TILE, TILE)
             res = dot(h[rows, :], wd[:, cols]) + prm[pl.ds(6, 1), cols]
             f[rows, cols] = res.astype(BF16)
@@ -293,7 +295,37 @@
             dr[rows, cols] = y.astype(BF16)
             return carry
 
-        lax.fori_loop(0, width // TILE, down, 0)
+        lax.fori_loop(0, width // TILE, body, 0)
+
+    def forward(mb):
+        def when_first(act):
+            pl.when(mb == 0)(act)
+
+        @pl.when(leading & (mb == 0))
+        def _():
+            for i in range(count):
+                load_x(i).wait()
+
+        @pl.when(trailing)
+        def _():
+            handed(mb).wait_recv()
+
+        norm_one(mb)
+        when_first(weight_copies[0].wait)
+        triple(mb)
+        attend(mb)
+        when_first(weight_copies[1].wait)
+        project(mb)
+        norm_two(mb)
+        when_first(weight_copies[2].wait)
+        up(mb)
+        when_first(weight_copies[3].wait)
+
+        @pl.when(trailing & (mb > 0))
+        def _():
+            out_copy(mb - 1).wait()
+
+        down(mb)
 
         @pl.when(leading)
         def _():
@@ -379,7 +411,6 @@
 
     def grad_attend(mb):
         rows = rows_of(mb)
-        lane = lax.broadcasted_iota(jnp.int32, (length, 128), 1) < HEAD
 
         def body(p, carry):
             qc, kc, vc = (ds(part * width + p * 128, 128) for part in range(3))
@@ -455,30 +486,271 @@
         def _():
             returned(mb).start()
 
-    def weight_grad(left, right, blocks, target, along_rows):
+    n_blocks = (3 * width + width + 2 * feed) // width
+    pieces = n_blocks // group
+    piece_rows = group * half
+    chunk = piece_rows // ring
+    staged = n_blocks * half
+
+    def remote(src, dst, send, recv, device):
+        return pltpu.make_async_remote_copy(
+            src_ref=src, dst_ref=dst, send_sem=send, recv_sem=recv, device_id=device, device_id_type=MESH
+        )
+
+    def twin_copy(block, slot):
+        return remote(
+            part.at[ds(staged + slot * half, half, 16)], twin_part.at[ds(block * half, half, 16)],
+            stage_send.at[slot], twin_recv.at[block], sibling,
+        )
+
+    def half_block(index, source):
+        piece, turn = index // (2 * group), index % (2 * group)
+        away = turn < group
+        block = piece * group + turn % group
+        slot = turn % 2
+        side = jnp.where(away, 1 - core, core)
+        base = pl.multiple_of(jnp.where(away, staged + slot * half, block * half), 16)
+
+        @pl.when(away & ((piece > 0) | (turn > 1)))
+        def _():
+            twin_copy(block, slot).wait_send()
+
+        source(block, side, base)
+
+        @pl.when(away)
+        def _():
+            twin_copy(block, slot).start()
+
+    def product(left, right, left_start, right_start, base):
+        lhs[...] = left[:, ds(left_start, half, 128)].T
+
+        def tile(n, inner):
+            part[pl.ds(base, half), ds(n * TILE, TILE)] = dot(
+                lhs[...], right[:, ds(right_start + n * TILE, TILE)]
+            ).astype(BF16)
+            return inner
+
+        lax.fori_loop(0, width // TILE, tile, 0)
+
+    per = feed // width
+
+    def from_down(block, side, base):
+        product(h, df, block * width + side * half, 0, base)
+
+    def from_up(block, side, base):
+        product(c, gp, side * half, (block - per) * width, base)
+
+    def from_rest(block, side, base):
+        pl.when(block == 2 * per)(lambda: product(o, dr, side * half, 0, base))
+        pl.when(block > 2 * per)(lambda: product(a, qkv, side * half, (block - 2 * per - 1) * width, base))
+
+    halves = 2 * per
+    first_tick = 2 * group
+
+    def weight_grad(phase, source):
         def body(i, carry):
-            block, part = i // 2, i % 2
-            if along_rows:
-                lhs[...] = left[:, ds(i * half, half)].T
-                r0, c0, rc0 = i * half, 0, 0
-            else:
-                lhs[...] = left[:, ds(part * half, half)].T
-                r0, c0, rc0 = part * half, block * width, block * width
-
-            def tile(n, inner):
-                cols = ds(n * TILE, TILE)
-                stage[:, cols] = dot(lhs[...], right[:, ds(rc0 + n * TILE, TILE)]).astype(BF16)
-                return inner
-
-            lax.fori_loop(0, width // TILE, tile, 0)
-            copy = pltpu.make_async_copy(
-                stage, target.at[ds(r0, half), ds(c0, width, 128)], stage_sem
-            )
-            copy.start()
-            copy.wait()
-            return carry
-
-        lax.fori_loop(0, 2 * blocks, body, 0)
+            index = phase * halves + i
+
+            @pl.when(index >= first_tick)
+            def _():
+                tick(index - first_tick)
+
+            half_block(index, source)
+            return carry
+
+        lax.fori_loop(0, halves, body, 0)
+
+    def where_rows(k, j):
+        return ds(k * piece_rows + j * chunk, chunk, 16)
+
+    def where_out(k, j):
+        offset = k * piece_rows + j * chunk
+        return ds((offset // half) * width + core * half + offset % half, chunk, 16)
+
+    def wrapped(index):
+        return lax.rem(index + 2 * ring, ring)
+
+    def sum_copy(k, d, s, j):
+        index = (k * 2 + d) * (ring - 1) + s
+        return remote(
+            part.at[where_rows(k, j), pl.ds(d * half, half)], arrived.at[index],
+            sum_send.at[index], sum_recv.at[index], neighbours[d],
+        )
+
+    def all_copy(k, d, s, j):
+        index = (k * 2 + d) * (ring - 1) + s
+        there = blocks.at[where_out(k, j), pl.ds(d * half, half)]
+        return remote(there, there, all_send.at[index], all_recv.at[index], neighbours[d])
+
+    def all_first(k, d, j):
+        index = (k * 2 + d) * (ring - 1)
+        return remote(
+            part.at[where_rows(k, j), pl.ds(d * half, half)], blocks.at[where_out(k, j), pl.ds(d * half, half)],
+            all_send.at[index], all_recv.at[index], neighbours[d],
+        )
+
+    def pair_copy(k, d, src, j):
+        index = k * 2 + d
+        return remote(
+            src, blocks.at[where_out(k, j), pl.ds(d * half, half)], pair_send.at[index], pair_recv.at[index], sibling
+        )
+
+    def own_copy(k, d, j):
+        return pltpu.make_async_copy(
+            part.at[where_rows(k, j), pl.ds(d * half, half)], blocks.at[where_out(k, j), pl.ds(d * half, half)],
+            own_sem.at[k * 2 + d],
+        )
+
+    def piece_event(k, e):
+        @pl.when(e == 0)
+        def _():
+            for b in range(group):
+                twin_copy(k * group + b, 0).wait_recv()
+
+            def combine(i, carry):
+                rr = ds(k * piece_rows + i * CHUNK, CHUNK)
+                part[rr, :] = (part[rr, :].astype(F32) + twin_part[rr, :].astype(F32)).astype(BF16)
+                return carry
+
+            lax.fori_loop(0, piece_rows // CHUNK, combine, 0)
+            for d in range(2):
+                sum_copy(k, d, 0, place).start()
+
+        @pl.when((e > 0) & (e < ring))
+        def _():
+            s = e - 1
+            for d, sign in ((0, 1), (1, -1)):
+                j = wrapped(place - sign * (s + 1))
+                sum_copy(k, d, s, j).wait_recv()
+                rr, cols = where_rows(k, j), pl.ds(d * half, half)
+                total = part[rr, cols].astype(F32) + arrived[(k * 2 + d) * (ring - 1) + s].astype(F32)
+                part[rr, cols] = total.astype(BF16)
+
+                @pl.when(e < ring - 1)
+                def _():
+                    sum_copy(k, d, e, j).start()
+
+                @pl.when(e == ring - 1)
+                def _():
+                    all_first(k, d, j).start()
+                    pair_copy(k, d, part.at[rr, cols], j).start()
+                    own_copy(k, d, j).start()
+
+        @pl.when(e >= ring)
+        def _():
+            s = e - ring
+            for d, sign in ((0, 1), (1, -1)):
+                j = wrapped(place - sign * s)
+                all_copy(k, d, s, j).wait_recv()
+
+                @pl.when(s < ring - 2)
+                def _():
+                    all_copy(k, d, s + 1, j).start()
+
+                pair_copy(k, d, blocks.at[where_out(k, j), pl.ds(d * half, half)], j).start()
+
+    events = 2 * ring - 1
+
+    def tick(t):
+        def body(k, carry):
+            e = t - k * 2 * group
+            pl.when((e >= 0) & (e < events))(lambda: piece_event(k, e))
+            return carry
+
+        lax.fori_loop(0, pieces, body, 0)
+
+    vhalf = ring * 8
+
+    def vrows(j):
+        return ds(core * vhalf + j * 8, 8)
+
+    def vpair_copy():
+        return remote(vpart.at[ds((1 - core) * vhalf, vhalf)], vtwin, vpair_send.at[0], vpair_recv.at[0], sibling)
+
+    def vsum_copy(s, j):
+        return remote(vpart.at[vrows(j)], varrived.at[s], vsum_send.at[s], vsum_recv.at[s], neighbours[0])
+
+    def vall_copy(s, j, src):
+        return remote(src.at[vrows(j)], vec.at[vrows(j)], vall_send.at[s], vall_recv.at[s], neighbours[0])
+
+    def vout_copy(src, rr):
+        return remote(src.at[rr], vec.at[rr], vpair_send.at[1], vpair_recv.at[1], sibling)
+
+    def vector_event(e):
+        @pl.when(e == 0)
+        def _():
+            vpair_copy().start()
+            vpair_copy().wait_recv()
+            rr = ds(core * vhalf, vhalf)
+            vpart[rr, :] = vpart[rr, :] + vtwin[...]
+            vsum_copy(0, place).start()
+
+        @pl.when((e > 0) & (e < ring))
+        def _():
+            j = wrapped(place - e)
+            vsum_copy(e - 1, j).wait_recv()
+            rr = vrows(j)
+            vpart[rr, :] = vpart[rr, :] + varrived[e - 1]
+
+            @pl.when(e < ring - 1)
+            def _():
+                vsum_copy(e, j).start()
+
+            @pl.when(e == ring - 1)
+            def _():
+                vec[rr, :] = vpart[rr, :]
+                vall_copy(0, j, vpart).start()
+
+        @pl.when(e >= ring)
+        def _():
+            s = e - ring
+            j = wrapped(place - s)
+            vall_copy(s, j, vec).wait_recv()
+
+            @pl.when(s < ring - 2)
+            def _():
+                vall_copy(s + 1, j, vec).start()
+
+            @pl.when(s == ring - 2)
+            def _():
+                vout_copy(vec, ds(core * vhalf, vhalf)).start()
+
+    def pack_vectors():
+        vpart[...] = jnp.zeros_like(vpart)
+        at = 0
+        for ref, size in [(acc.at[row], width) for row in range(8)] + [(acc_t, 3 * width), (acc_f, feed)]:
+            for i in range(size // 128):
+                vpart[pl.ds(at, 1), :] = jnp.sum(ref[:, pl.ds(i * 128, 128)], axis=0, keepdims=True)
+                at += 1
+
+    def finish():
+        for d in range(2):
+            def body(k, carry):
+                whole = blocks.at[ds(k * piece_rows, piece_rows, 16), pl.ds(d * half, half)]
+                index = k * 2 + d
+                remote(whole, whole, pair_send.at[index], pair_recv.at[index], sibling).wait()
+                own_copy(k, d, 0).wait()
+
+                def sends(s, inner):
+                    sum_copy(k, d, s, 0).wait_send()
+                    all_copy(k, d, s, 0).wait_send()
+                    return inner
+
+                return lax.fori_loop(0, ring - 1, sends, carry)
+
+            lax.fori_loop(0, pieces, body, 0)
+
+        def vsends(s, carry):
+            vsum_copy(s, 0).wait_send()
+            vall_copy(s, 0, vec).wait_send()
+            return carry
+
+        lax.fori_loop(0, ring - 1, vsends, 0)
+        vpair_copy().wait_send()
+        vout_copy(vec, ds(core * vhalf, vhalf)).wait_send()
+        vout_copy(vec, ds((1 - core) * vhalf, vhalf)).wait_recv()
+        for slot in range(2):
+            twin_copy(0, slot).wait_send()
 
     def slot_body(slot, carry):
         one, two = schedules(count)
@@ -486,18 +758,24 @@
         mb = jnp.where(leading, picked([e[1] for e in one], slot), picked([e[1] for e in two], slot))
         for which, act in ((FWD, forward), (DF, grad_f), (DU, grad_u), (DM, grad_m), (ATT, grad_attend), (DX, grad_x)):
             pl.when(phase == which)(functools.partial(act, mb))
-        pl.when(phase == WD)(lambda: weight_grad(h, df, feed // width, gwd, True))
-        pl.when(phase == WU)(lambda: weight_grad(c, gp, feed // width, gwu, False))
-        pl.when(phase == WO)(lambda: weight_grad(o, dr, 1, gwo, False))
-        pl.when(phase == WT)(lambda: weight_grad(a, qkv, 3, gwt, False))
+        for number, (which, source) in enumerate(((WD, from_down), (WU, from_up), (WT, from_rest))):
+            pl.when(phase == which)(functools.partial(weight_grad, number, source))
         return carry
 
     lax.fori_loop(0, len(schedules(count)[0]), slot_body, 0)
-
-    for row in range(8):
-        vec[pl.ds(row, 1), pl.ds(0, width)] = jnp.sum(acc[row], axis=0, keepdims=True)
-    vec[pl.ds(8, 1), pl.ds(0, 3 * width)] = jnp.sum(acc_t[...], axis=0, keepdims=True)
-    vec[pl.ds(9, 1), :] = jnp.sum(acc_f[...], axis=0, keepdims=True)
+    pack_vectors()
+
+    last_tick = (pieces - 1) * 2 * group + events
+    start_tick = 2 * n_blocks - first_tick
+
+    def drain(t, carry):
+        tick(t)
+        e = t - start_tick - 1
+        pl.when((e >= 0) & (e < events))(lambda: vector_event(e))
+        return carry
+
+    lax.fori_loop(start_tick, max(last_tick, start_tick + 1 + events), drain, 0)
+    finish()
 
     @pl.when(leading)
     def _():
@@ -507,6 +785,50 @@
     def _():
         for i in range(count):
             returned(i).wait_send()
+
+
+def widen_kernel(per, source, gwd, gwu, gwo, gwt):
+    block = pl.program_id(0)
+    for target, first, after in ((gwd, 0, per), (gwu, per, 2 * per), (gwo, 2 * per, 2 * per + 1), (gwt, 2 * per + 1, 2 * per + 4)):
+
+        @pl.when((block >= first) & (block < after))
+        def _():
+            target[...] = source[...].astype(F32)
+
+
+def widened(blocks, width, per):
+    half = width // 2
+
+    def rows_down(i, part):
+        return (jnp.where(i < per, 2 * i + part, 2 * per - 1), 0)
+
+    def beside(first, number):
+        def index(i, part):
+            inside = jnp.clip(i - first, 0, number - 1)
+            side = jnp.where(i < first, 0, jnp.where(i >= first + number, 1, part))
+            return (side, inside)
+
+        return index
+
+    shape = (half, width)
+    return pl.pallas_call(
+        functools.partial(widen_kernel, per),
+        grid=(2 * per + 4, 2),
+        in_specs=[pl.BlockSpec(shape, lambda i, part: (2 * i + part, 0))],
+        out_specs=(
+            pl.BlockSpec(shape, rows_down),
+            pl.BlockSpec(shape, beside(per, per)),
+            pl.BlockSpec(shape, beside(2 * per, 1)),
+            pl.BlockSpec(shape, beside(2 * per + 1, 3)),
+        ),
+        out_shape=(
+            jax.ShapeDtypeStruct((per * width, width), F32),
+            jax.ShapeDtypeStruct((width, per * width), F32),
+            jax.ShapeDtypeStruct((width, width), F32),
+            jax.ShapeDtypeStruct((width, 3 * width), F32),
+        ),
+        compiler_params=pltpu.CompilerParams(vmem_limit_bytes=60 << 20),
+    )(blocks)
 
 
 def local(
@@ -517,22 +839,28 @@
     count, length, width = block_io.shape[1:]
     feed = up_weight.shape[2]
     rows = count * length
+    half = width // 2
+    lines, depth = lax.axis_size("dp") // 2, lax.axis_size("inner")
+    ring = lines * depth
+    n_blocks = (4 * width + 2 * feed) // width
+    group = 2 if (2 * half) % (16 * ring) == 0 else feed // width
+    pieces = n_blocks // group
+    streams = pieces * 2 * (ring - 1)
+    chunk = group * half // ring
     key_code = jnp.where(valid_tokens == 1, segments, -1)[:, :, None]
     query_code = segments[:, None, :]
     any_spec = pl.BlockSpec(memory_space=pl.ANY)
     vmem = pl.BlockSpec(memory_space=pltpu.VMEM)
-    outs = pl.pallas_call(
-        functools.partial(kernel, count, length, width, feed),
+    sem = pltpu.SemaphoreType.DMA
+    ends, blocks, vec = pl.pallas_call(
+        functools.partial(kernel, count, length, width, feed, lines, depth, group),
         out_shape=(
             jax.ShapeDtypeStruct((count, length, width), F32),
-            jax.ShapeDtypeStruct((width, 3 * width), BF16),
-            jax.ShapeDtypeStruct((width, width), BF16),
-            jax.ShapeDtypeStruct((width, feed), BF16),
-            jax.ShapeDtypeStruct((feed, width), BF16),
-            jax.ShapeDtypeStruct((16, feed), F32),
+            jax.ShapeDtypeStruct((n_blocks * width, width), BF16),
+            jax.ShapeDtypeStruct((2 * ring * 8, 128), F32),
         ),
         in_specs=[any_spec] + [vmem] * 12 + [any_spec] * 4,
-        out_specs=(any_spec,) * 5 + (vmem,),
+        out_specs=(any_spec, any_spec, vmem),
         scratch_shapes=[
             pltpu.VMEM((width, 3 * width), BF16),
             pltpu.VMEM((width, width), BF16),
@@ -559,44 +887,67 @@
             pltpu.VMEM((8, 8, width), F32),
             pltpu.VMEM((8, feed), F32),
             pltpu.VMEM((8, 3 * width), F32),
-            pltpu.VMEM((width // 2, rows), BF16),
-            pltpu.VMEM((width // 2, width), BF16),
-            pltpu.SemaphoreType.DMA((4 + count,)),
-            pltpu.SemaphoreType.DMA,
-            pltpu.SemaphoreType.DMA,
-            pltpu.SemaphoreType.DMA((count,)),
-            pltpu.SemaphoreType.DMA((count,)),
+            pltpu.VMEM((half, rows), BF16),
+            pltpu.VMEM((n_blocks * half + 2 * half, width), BF16),
+            pltpu.VMEM((n_blocks * half, width), BF16),
+            pltpu.VMEM((streams, chunk, half), BF16),
+            pltpu.VMEM((2 * ring * 8, 128), F32),
+            pltpu.VMEM((ring * 8, 128), F32),
+            pltpu.VMEM((ring - 1, 8, 128), F32),
+            sem((4 + count,)),
+            sem,
+            sem((count,)),
+            sem((count,)),
+            sem((2,)),
+            sem((n_blocks,)),
+            sem((streams,)),
+            sem((streams,)),
+            sem((streams,)),
+            sem((streams,)),
+            sem((2 * pieces,)),
+            sem((2 * pieces,)),
+            sem((2 * pieces,)),
+            sem((ring - 1,)),
+            sem((ring - 1,)),
+            sem((ring - 1,)),
+            sem((ring - 1,)),
+            sem((2,)),
+            sem((2,)),
         ],
         compiler_params=pltpu.CompilerParams(
-            collective_id=0, has_side_effects=True, vmem_limit_bytes=62 << 20
+            collective_id=0, has_side_effects=True, vmem_limit_bytes=63 << 20
         ),
     )(
         block_io[0], key_code, query_code, attention_gain, attention_shift, triple_bias, output_bias,
         attention_scale, feed_gain, feed_shift, up_bias, down_bias, feed_scale,
         triple_weight[0], output_weight[0], up_weight[0], down_weight[0],
     )
-    ends, gwt, gwo, gwu, gwd, vec = outs
-    gwt, gwo, gwu, gwd, vec = lax.psum((gwt, gwo, gwu, gwd, vec), ("dp", "inner"))
-
-    def row(index):
-        return vec[index : index + 1, :width]
-
+    per = feed // width
+    gwd, gwu, gwo, gwt = widened(blocks, width, per)
+
+    flat = vec.reshape(-1)
+    vectors = []
+    at = 0
+    for size in [width] * 8 + [3 * width, feed]:
+        vectors.append(flat[at : at + size][None])
+        at += size
+    ga, gs, gob, gasc, gfg, gfs, gdb, gfsc, gtb, gub = vectors
     return (
         ends[None],
-        row(0),
-        row(1),
-        gwt.astype(F32)[None],
-        jnp.concatenate([vec[8:9, :width], vec[8:9, 2 * width : 3 * width]], axis=1),
-        gwo.astype(F32)[None],
-        row(2),
-        row(3),
-        row(4),
-        row(5),
-        gwu.astype(F32)[None],
-        vec[9:10, :],
-        gwd.astype(F32)[None],
-        row(6),
-        row(7),
+        ga,
+        gs,
+        gwt[None],
+        jnp.concatenate([gtb[:, :width], gtb[:, 2 * width :]], axis=1),
+        gwo[None],
+        gob,
+        gasc,
+        gfg,
+        gfs,
+        gwu[None],
+        gub,
+        gwd[None],
+        gdb,
+        gfsc,
     )
 
 

time: 601 us -> 360 us (0.60)
  waiting for transfers between devices: 348 us -> 0 us
  Pallas kernels: 213 us -> 349 us
  other arithmetic: 18.4 us -> 1.31 us
  between operations: 14.1 us -> 0.67 us
    psum x2 -> x0, waiting for transfers between devices: 348 us -> none  [local(): lax.psum((gwt, gwo, gwu, gwd, vec), ('dp', 'inner'))]
    pallas_call x1 -> x2, Pallas kernels: 213 us -> 349 us  [the longest x1 326 us: local(): pl.pallas_call(functools.partial(kernel, count, length, width, feed, line...]
    broadcast_in_dim x4 -> x0, other arithmetic: 17.1 us -> none  [the longest x1 7.52 us: local(): gwu.astype(F32)[None]]
  transfers between devices with their start and end apart: 2 -> 0, of which waited for: 2 -> 0; matrix products, arithmetic and copies ran while one was open for 1% -> 0% of each run, Pallas kernels for 0% -> 0%
where the time goes in v2:
time: 360 us; the launch traced here: 359 us
  Pallas kernels  349 us (97%)
  local copies, waits for them, and re-layouts  8.62 us (2%)
    pallas_call x1, Pallas kernels, local(): pl.pallas_call(functools.partial(kernel, count, length, width, feed, line...  326 us
    pallas_call x1, Pallas kernels, widened(): pl.pallas_call(functools.partial(widen_kernel, per), grid=(2 * per + 4, 2...  22.7 us

profile of v2, /device:TPU:0, one launch (start us, length us, event | category | flops | bytes accessed | tf_op | source)
XLA Modules:
  0.0 359.3 jit_solution(10525865066511743039)
XLA Ops:
  0.6 0.7 fusion
  1.4 1.3 broadcast_in_dim.57.query_code
  2.6 0.9 copy.32.key_code
  3.5 326.0 %shard_map.280 = (f32[2,320,768]{2,1,0:T(8,128)}, bf16[9216,768]{1,0:T(8,128)(2,1)}, f32[128,128]{1,0:T(8,128)}) custom-call(bf16[2,320,768]{2,1,0:T(8,128)(2,1)} %bitcast.64, s32[2,320,1]{2,1,0:T(8,128)} %copy.32.key_code, s32[2,1,320]{2,1,0:T(1,128)} %broadcast_in_dim.57.query_code, bf16[1,768]{1,0:T(2,128)(2,1)} %ag.1, bf16[1,768]{1,0:T(2,128)(2,1)} %ash.1, ...), custom_call_target="tpu_custom_call" | custom-call | tf_op jit(solution)/shard_map/pallas_call | solution.py:855
  329.5 0.7 slice_bitcast_fusion
  330.3 0.6 pad_maximum_fusion
  330.9 1.3 slice.55
  332.2 0.8 slice_bitcast_fusion.1
  333.0 0.6 copy_bitcast_fusion.1
  333.6 0.6 copy_bitcast_fusion.3
  334.1 0.6 copy_bitcast_fusion.5
  334.7 0.6 copy_bitcast_fusion.7
  335.3 0.0 copy-start
  335.3 22.7 %shard_map.281 = (f32[3072,768]{1,0:T(8,128)}, f32[768,3072]{1,0:T(8,128)}, f32[768,768]{1,0:T(8,128)}, f32[768,2304]{1,0:T(8,128)}) custom-call(bf16[9216,768]{1,0:T(8,128)(2,1)} %get-tuple-element.24.source), custom_call_target="tpu_custom_call" | custom-call | tf_op jit(solution)/shard_map/pallas_call | solution.py:814
  358.0 0.0 copy-done
  358.0 1.3 copy.53
  (2 shorter events, 0.0 us)
Async XLA Ops:
  335.3 22.7 %copy-start = (f32[2,320,768]{2,1,0:T(8,128)S(1)}, f32[2,320,768]{2,1,0:T(8,128)}, u32[]{:S(2)}) copy-start(f32[2,320,768]{2,1,0:T(8,128)} %get-tuple-element.22) | copy-start | bytes 5898244

commit v3 on v2

--- a/solution.py
+++ b/solution.py
@@ -13,24 +13,13 @@
 MESH = pl.DeviceIdType.MESH
 F32 = jnp.float32
 BF16 = jnp.bfloat16
-CHUNK = 32
-TILE = 256
+CHUNK = 320
+TILE = 768
 
 FWD, DF, DU, DM, ATT, DX, WD, WU, WT = range(9)
 
-TAIL = 0.305
-POLY = (
-    0.12163973599672318,
-    0.12246681749820709,
-    0.10342079401016235,
-    0.1210220605134964,
-    -0.037977732717990875,
-    0.18571804463863373,
-    -0.15298904478549957,
-    0.03669937700033188,
-)
-
 NT = (((1,), (1,)), ((), ()))
+TN = (((0,), (0,)), ((), ()))
 
 
 def nt_dot(left, right):
@@ -39,6 +28,10 @@
 
 def dot(left, right):
     return jnp.dot(left, right, preferred_element_type=F32)
+
+
+def tn_dot(left, right):
+    return lax.dot_general(left, right, TN, preferred_element_type=F32)
 
 
 def ds(start, size, multiple=None):
@@ -66,15 +59,9 @@
 
 
 def gelu_pair(values):
-    size = jnp.abs(values)
-    bell = jnp.exp(-0.5 * values * values)
-    t = 1.0 / (1.0 + TAIL * size)
-    acc = jnp.full_like(t, POLY[-1])
-    for c in POLY[-2::-1]:
-        acc = acc * t + c
-    tail = acc * t * bell
-    phi = jnp.where(values >= 0, 1.0 - tail, tail)
-    return values * phi, phi + values * (bell * 0.3989422804014327)
+    phi = 0.5 + 0.5 * lax.erf(values * 0.7071067811865476)
+    bell = jnp.exp(-0.5 * values * values) * 0.3989422804014327
+    return values * phi, phi + values * bell
 
 
 def picked(table, slot):
@@ -99,11 +86,25 @@
     return first, second
 
 
+def tick_plan(slots, per_phase):
+    tick, bases, after, starts = 0, [], [], []
+    for phase, unused in slots:
+        bases.append(tick)
+        if phase in (WD, WU, WT):
+            starts += [tick + i for i in range(per_phase)]
+            tick += per_phase
+            after.append(1)
+        else:
+            after.append(1 if starts and phase != DX else 0)
+            tick += after[-1]
+    return bases, after, starts, tick
+
+
 def kernel(
     count, length, width, feed, lines, depth, group,
     data, key_code, query_code, ag, ash, tb, ob, asc, fg, fsh, ub, db, fsc, wt_h, wo_h, wu_h, wd_h,
     ends, blocks, vec,
-    wt, wo, wu, wd, x, a, qkv, o, r, m, c, gp, h, f, g, df, dr, tmp, outb, bias, lse, prm, acc, acc_f, acc_t, lhs,
+    wt, wo, wu, wd, x, a, qkv, o, r, m, c, gp, h, f, g, dr, tmp, bias, lse, prm, acc, acc_f, acc_t, lhs,
     part, twin_part, arrived, vpart, vtwin, varrived,
     load_sem, out_sem, send_sem, recv_sem, stage_send, twin_recv,
     sum_send, sum_recv, all_send, all_recv, pair_send, pair_recv, own_sem,
@@ -149,7 +150,7 @@
         )
 
     def out_copy(mb):
-        return pltpu.make_async_copy(outb, ends.at[mb], out_sem)
+        return pltpu.make_async_copy(tmp, ends.at[mb], out_sem)
 
     @pl.when(leading)
     def _():
@@ -200,7 +201,8 @@
         own = lax.broadcasted_iota(jnp.int32, (length, length), 0) == lax.broadcasted_iota(
             jnp.int32, (length, length), 1
         )
-        bias[i] = jnp.where(same | own, 0.0, -1000000000.0)
+        banned = jnp.where(same | own, 0.0, -1000000000.0)
+        bias[i] = jnp.concatenate([banned, banned], axis=1).astype(BF16)
 
     pl.semaphore_wait(barrier, 4)
 
@@ -225,26 +227,27 @@
 
         lax.fori_loop(0, 3 * width // TILE, body, 0)
 
+    def two_heads(values):
+        zero = jnp.zeros_like(values)
+        return jnp.concatenate([jnp.where(lane, values, zero), jnp.where(lane, zero, values)], axis=0)
+
+    def merged(values):
+        return jnp.where(lane, values[:length], values[length:])
+
     def attend(mb):
         rows = rows_of(mb)
 
         def body(p, carry):
-            q = qkv[rows, ds(p * 128, 128)]
+            q = qkv[rows, ds(p * 128, 128)] * SCALE
             k = qkv[rows, ds(width + p * 128, 128)]
             v = qkv[rows, ds(2 * width + p * 128, 128)]
-            zero = jnp.zeros_like(q)
-            vt = v.T
-            outs = []
-            for hh in range(2):
-                qm = jnp.where(lane, q, zero) if hh == 0 else jnp.where(lane, zero, q)
-                s = nt_dot(k, qm) * SCALE + bias[mb]
-                top = jnp.max(s, axis=0, keepdims=True)
-                e = jnp.exp(s - top)
-                total = jnp.sum(e, axis=0, keepdims=True)
-                prob = (e * (1.0 / total)).astype(BF16)
-                lse[mb, 2 * p + hh] = top + jnp.log(total)
-                outs.append(dot(vt[hh * HEAD : (hh + 1) * HEAD], prob))
-            o[rows, ds(p * 128, 128)] = jnp.concatenate(outs, axis=0).T.astype(BF16)
+            s = nt_dot(k, two_heads(q)) + bias[mb].astype(F32)
+            top = jnp.max(s, axis=0, keepdims=True)
+            e = jnp.exp(s - top)
+            total = jnp.sum(e, axis=0, keepdims=True)
+            lse[mb, p] = top + jnp.log(total)
+            prob = (e * (1.0 / total)).astype(BF16)
+            o[rows, ds(p * 128, 128)] = merged(tn_dot(prob, v)).astype(BF16)
             return carry
 
         lax.fori_loop(0, pairs, body, 0)
@@ -291,7 +294,7 @@
             res = dot(h[rows, :], wd[:, cols]) + prm[pl.ds(6, 1), cols]
             f[rows, cols] = res.astype(BF16)
             y = m[rows, cols] + prm[pl.ds(7, 1), cols] * res
-            outb[:, cols] = y
+            tmp[:, cols] = y
             dr[rows, cols] = y.astype(BF16)
             return carry
 
@@ -321,10 +324,6 @@
         up(mb)
         when_first(weight_copies[3].wait)
 
-        @pl.when(trailing & (mb > 0))
-        def _():
-            out_copy(mb - 1).wait()
-
         down(mb)
 
         @pl.when(leading)
@@ -353,7 +352,7 @@
             up_grad = g[rr, :].astype(F32)
             add_acc(7, up_grad * f[rr, :].astype(F32))
             value = (up_grad * param(7)).astype(BF16)
-            df[rr, :] = value
+            f[rr, :] = value
             add_acc(6, value.astype(F32))
             return carry
 
@@ -364,7 +363,7 @@
 
         def body(n, carry):
             cols = ds(n * TILE, TILE)
-            value = (nt_dot(df[rows, :], wd[cols, :]) * gp[rows, cols].astype(F32)).astype(BF16)
+            value = (nt_dot(f[rows, :], wd[cols, :]) * gp[rows, cols].astype(F32)).astype(BF16)
             gp[rows, cols] = value
             acc_f[:, cols] += folded(value.astype(F32))
             return carry
@@ -378,6 +377,10 @@
         def _():
             for i in range(count):
                 handed(i).wait_send()
+
+        @pl.when(trailing | (mb > 0))
+        def _():
+            out_copy(jnp.where(leading, mb - 1, mb)).wait()
 
         def first(n, carry):
             cols = ds(n * TILE, TILE)
@@ -414,26 +417,16 @@
 
         def body(p, carry):
             qc, kc, vc = (ds(part * width + p * 128, 128) for part in range(3))
-            q, k, v, do = qkv[rows, qc], qkv[rows, kc], qkv[rows, vc], g[rows, qc]
-            zero = jnp.zeros_like(q)
-            kt = k.T
-            dq = []
-            dk = jnp.zeros((length, 128), F32)
-            dv = jnp.zeros((length, 128), F32)
-            for hh in range(2):
-                qm = jnp.where(lane, q, zero) if hh == 0 else jnp.where(lane, zero, q)
-                dom = jnp.where(lane, do, zero) if hh == 0 else jnp.where(lane, zero, do)
-                s = nt_dot(k, qm) * SCALE + bias[mb]
-                prob = jnp.exp(s - lse[mb, 2 * p + hh])
-                dv = dv + dot(prob.astype(BF16), dom)
-                dp = nt_dot(v, dom)
-                inner = jnp.sum(prob * dp, axis=0, keepdims=True)
-                grad = (prob * (dp - inner)).astype(BF16)
-                dk = dk + dot(grad, qm)
-                dq.append(dot(kt[hh * HEAD : (hh + 1) * HEAD], grad))
-            dq = (jnp.concatenate(dq, axis=0).T * SCALE).astype(BF16)
-            dk = (dk * SCALE).astype(BF16)
-            dv = dv.astype(BF16)
+            q = two_heads(qkv[rows, qc] * SCALE)
+            do = two_heads(g[rows, qc])
+            k, v = qkv[rows, kc], qkv[rows, vc]
+            prob = jnp.exp(nt_dot(k, q) + bias[mb].astype(F32) - lse[mb, p])
+            dv = dot(prob.astype(BF16), do).astype(BF16)
+            dp = nt_dot(v, do)
+            inner = jnp.sum(prob * dp, axis=0, keepdims=True)
+            grad = (prob * (dp - inner)).astype(BF16)
+            dk = dot(grad, q).astype(BF16)
+            dq = (merged(tn_dot(grad, k)) * SCALE).astype(BF16)
             qkv[rows, qc] = dq
             qkv[rows, kc] = dk
             qkv[rows, vc] = dv
@@ -452,14 +445,6 @@
             return carry
 
         lax.fori_loop(0, width // TILE, first, 0)
-
-        @pl.when(leading & (mb > 0))
-        def _():
-            out_copy(mb - 1).wait()
-
-        @pl.when(trailing & (mb == count - 1))
-        def _():
-            out_copy(mb).wait()
 
         def body(i, carry):
             rr = chunk_rows(mb, i)
@@ -471,7 +456,7 @@
 
             @pl.when(leading)
             def _():
-                outb[ds(i * CHUNK, CHUNK), :] = total
+                tmp[ds(i * CHUNK, CHUNK), :] = total
 
             g[rr, :] = total.astype(BF16)
             return carry
@@ -490,6 +475,12 @@
     pieces = n_blocks // group
     piece_rows = group * half
     chunk = piece_rows // ring
+    slots = schedules(count)
+    plans = [tick_plan(entry, pieces // 3) for entry in slots]
+
+    def chosen(what, index):
+        return jnp.where(leading, picked(plans[0][what], index), picked(plans[1][what], index))
+
     staged = n_blocks * half
 
     def remote(src, dst, send, recv, device):
@@ -535,7 +526,7 @@
     per = feed // width
 
     def from_down(block, side, base):
-        product(h, df, block * width + side * half, 0, base)
+        product(h, f, block * width + side * half, 0, base)
 
     def from_up(block, side, base):
         product(c, gp, side * half, (block - per) * width, base)
@@ -545,17 +536,14 @@
         pl.when(block > 2 * per)(lambda: product(a, qkv, side * half, (block - 2 * per - 1) * width, base))
 
     halves = 2 * per
-    first_tick = 2 * group
-
-    def weight_grad(phase, source):
+
+    def weight_grad(phase, source, base):
         def body(i, carry):
-            index = phase * halves + i
-
-            @pl.when(index >= first_tick)
+            @pl.when((i > 0) & (lax.rem(i, 2 * group) == 0))
             def _():
-                tick(index - first_tick)
-
-            half_block(index, source)
+                tick(base + i // (2 * group) - 1)
+
+            half_block(phase * halves + i, source)
             return carry
 
         lax.fori_loop(0, halves, body, 0)
@@ -608,11 +596,11 @@
                 twin_copy(k * group + b, 0).wait_recv()
 
             def combine(i, carry):
-                rr = ds(k * piece_rows + i * CHUNK, CHUNK)
+                rr = ds(k * piece_rows + i * half, half)
                 part[rr, :] = (part[rr, :].astype(F32) + twin_part[rr, :].astype(F32)).astype(BF16)
                 return carry
 
-            lax.fori_loop(0, piece_rows // CHUNK, combine, 0)
+            lax.fori_loop(0, group, combine, 0)
             for d in range(2):
                 sum_copy(k, d, 0, place).start()
 
@@ -653,7 +641,7 @@
 
     def tick(t):
         def body(k, carry):
-            e = t - k * 2 * group
+            e = t - chosen(2, k)
             pl.when((e >= 0) & (e < events))(lambda: piece_event(k, e))
             return carry
 
@@ -753,28 +741,28 @@
             twin_copy(0, slot).wait_send()
 
     def slot_body(slot, carry):
-        one, two = schedules(count)
-        phase = jnp.where(leading, picked([e[0] for e in one], slot), picked([e[0] for e in two], slot))
-        mb = jnp.where(leading, picked([e[1] for e in one], slot), picked([e[1] for e in two], slot))
+        phase = jnp.where(leading, picked([e[0] for e in slots[0]], slot), picked([e[0] for e in slots[1]], slot))
+        mb = jnp.where(leading, picked([e[1] for e in slots[0]], slot), picked([e[1] for e in slots[1]], slot))
+        base = chosen(0, slot)
         for which, act in ((FWD, forward), (DF, grad_f), (DU, grad_u), (DM, grad_m), (ATT, grad_attend), (DX, grad_x)):
             pl.when(phase == which)(functools.partial(act, mb))
         for number, (which, source) in enumerate(((WD, from_down), (WU, from_up), (WT, from_rest))):
-            pl.when(phase == which)(functools.partial(weight_grad, number, source))
+            pl.when(phase == which)(functools.partial(weight_grad, number, source, base))
+        inner = jnp.where(phase >= WD, pieces // 3 - 1, 0)
+        pl.when(chosen(1, slot) == 1)(lambda: tick(base + inner))
         return carry
 
-    lax.fori_loop(0, len(schedules(count)[0]), slot_body, 0)
+    lax.fori_loop(0, len(slots[0]), slot_body, 0)
     pack_vectors()
-
-    last_tick = (pieces - 1) * 2 * group + events
-    start_tick = 2 * n_blocks - first_tick
-
-    def drain(t, carry):
+    start = jnp.where(leading, plans[0][3], plans[1][3])
+
+    def drain(i, carry):
+        t = start + i
         tick(t)
-        e = t - start_tick - 1
-        pl.when((e >= 0) & (e < events))(lambda: vector_event(e))
+        pl.when(i < events)(lambda: vector_event(i))
         return carry
 
-    lax.fori_loop(start_tick, max(last_tick, start_tick + 1 + events), drain, 0)
+    lax.fori_loop(0, events, drain, 0)
     finish()
 
     @pl.when(leading)
@@ -797,26 +785,16 @@
 
 
 def widened(blocks, width, per):
-    half = width // 2
-
-    def rows_down(i, part):
-        return (jnp.where(i < per, 2 * i + part, 2 * per - 1), 0)
-
     def beside(first, number):
-        def index(i, part):
-            inside = jnp.clip(i - first, 0, number - 1)
-            side = jnp.where(i < first, 0, jnp.where(i >= first + number, 1, part))
-            return (side, inside)
-
-        return index
-
-    shape = (half, width)
+        return lambda i: (0, jnp.clip(i - first, 0, number - 1))
+
+    shape = (width, width)
     return pl.pallas_call(
         functools.partial(widen_kernel, per),
-        grid=(2 * per + 4, 2),
-        in_specs=[pl.BlockSpec(shape, lambda i, part: (2 * i + part, 0))],
+        grid=(2 * per + 4,),
+        in_specs=[pl.BlockSpec(shape, lambda i: (i, 0))],
         out_specs=(
-            pl.BlockSpec(shape, rows_down),
+            pl.BlockSpec(shape, lambda i: (jnp.minimum(i, per - 1), 0)),
             pl.BlockSpec(shape, beside(per, per)),
             pl.BlockSpec(shape, beside(2 * per, 1)),
             pl.BlockSpec(shape, beside(2 * per + 1, 3)),
@@ -878,11 +856,9 @@
             pltpu.VMEM((rows, width), BF16),
             pltpu.VMEM((rows, width), BF16),
             pltpu.VMEM((rows, width), BF16),
-            pltpu.VMEM((rows, width), BF16),
             pltpu.VMEM((length, width), F32),
-            pltpu.VMEM((length, width), F32),
-            pltpu.VMEM((count, length, length), F32),
-            pltpu.VMEM((count, HEADS, 1, length), F32),
+            pltpu.VMEM((count, length, 2 * length), BF16),
+            pltpu.VMEM((count, HEADS // 2, 1, 2 * length), F32),
             pltpu.VMEM((16, feed), F32),
             pltpu.VMEM((8, 8, width), F32),
             pltpu.VMEM((8, feed), F32),

time: 360 us -> 283 us (0.79)
  Pallas kernels: 349 us -> 272 us
    pallas_call x1, Pallas kernels: 326 us -> 254 us  [local(): pl.pallas_call(functools.partial(kernel, count, length, width, feed, line...]
    pallas_call x1, Pallas kernels: 22.7 us -> 17.9 us  [widened(): pl.pallas_call(functools.partial(widen_kernel, per), grid=(2 * per + 4,),...]
where the time goes in v3:
time: 283 us
  Pallas kernels  272 us (96%)
  local copies, waits for them, and re-layouts  8.62 us (3%)
    pallas_call x1, Pallas kernels, local(): pl.pallas_call(functools.partial(kernel, count, length, width, feed, line...  254 us
    pallas_call x1, Pallas kernels, widened(): pl.pallas_call(functools.partial(widen_kernel, per), grid=(2 * per + 4,),...  17.9 us

profile of v3, /device:TPU:0, one launch (start us, length us, event | category | flops | bytes accessed | tf_op | source)
XLA Modules:
  0.0 282.5 jit_solution(5220501841686769439)
XLA Ops:
  0.6 0.7 fusion
  1.4 1.3 broadcast_in_dim.57.query_code
  2.6 0.9 copy.32.key_code
  3.5 254.0 %shard_map.280 = (f32[2,320,768]{2,1,0:T(8,128)}, bf16[9216,768]{1,0:T(8,128)(2,1)}, f32[128,128]{1,0:T(8,128)}) custom-call(bf16[2,320,768]{2,1,0:T(8,128)(2,1)} %bitcast.64, s32[2,320,1]{2,1,0:T(8,128)} %copy.32.key_code, s32[2,1,320]{2,1,0:T(1,128)} %broadcast_in_dim.57.query_code, bf16[1,768]{1,0:T(2,128)(2,1)} %ag.1, bf16[1,768]{1,0:T(2,128)(2,1)} %ash.1, ...), custom_call_target="tpu_custom_call" | custom-call | tf_op jit(solution)/shard_map/pallas_call | solution.py:833
  257.5 0.7 slice_bitcast_fusion
  258.3 0.6 pad_maximum_fusion
  258.9 1.3 slice.55
  260.2 0.8 slice_bitcast_fusion.1
  261.0 0.6 copy_bitcast_fusion.1
  261.6 0.6 copy_bitcast_fusion.3
  262.2 0.6 copy_bitcast_fusion.5
  262.7 0.6 copy_bitcast_fusion.7
  263.3 0.0 copy-start
  263.3 17.9 %shard_map.281 = (f32[3072,768]{1,0:T(8,128)}, f32[768,3072]{1,0:T(8,128)}, f32[768,768]{1,0:T(8,128)}, f32[768,2304]{1,0:T(8,128)}) custom-call(bf16[9216,768]{1,0:T(8,128)(2,1)} %get-tuple-element.24.source), custom_call_target="tpu_custom_call" | custom-call | tf_op jit(solution)/shard_map/pallas_call | solution.py:792
  281.2 0.0 copy-done
  281.2 1.3 copy.53
  (2 shorter events, 0.0 us)
Async XLA Ops:
  263.3 17.9 %copy-start = (f32[2,320,768]{2,1,0:T(8,128)S(1)}, f32[2,320,768]{2,1,0:T(8,128)}, u32[]{:S(2)}) copy-start(f32[2,320,768]{2,1,0:T(8,128)} %get-tuple-element.22) | copy-start | bytes 5898244

commit v4 on v3

--- a/solution.py
+++ b/solution.py
@@ -15,6 +15,9 @@
 BF16 = jnp.bfloat16
 CHUNK = 320
 TILE = 768
+PAIRS = 6
+BACK_PAIRS = 6
+WIDE = 3072
 
 FWD, DF, DU, DM, ATT, DX, WD, WU, WT = range(9)
 
@@ -102,7 +105,7 @@
 
 def kernel(
     count, length, width, feed, lines, depth, group,
-    data, key_code, query_code, ag, ash, tb, ob, asc, fg, fsh, ub, db, fsc, wt_h, wo_h, wu_h, wd_h,
+    data, segment, valid, ag, ash, tb, ob, asc, fg, fsh, ub, db, fsc, wt_h, wo_h, wu_h, wd_h,
     ends, blocks, vec,
     wt, wo, wu, wd, x, a, qkv, o, r, m, c, gp, h, f, g, dr, tmp, bias, lse, prm, acc, acc_f, acc_t, lhs,
     part, twin_part, arrived, vpart, vtwin, varrived,
@@ -197,7 +200,9 @@
     acc_t[...] = jnp.zeros_like(acc_t)
 
     for i in range(count):
-        same = key_code[i] == query_code[i]
+        number = segment[pl.ds(i, 1), :]
+        code = jnp.where(valid[pl.ds(i, 1), :] == 1, number, -1).astype(F32)
+        same = jnp.broadcast_to(code, (128, length)).T[:, :1] == number.astype(F32)
         own = lax.broadcasted_iota(jnp.int32, (length, length), 0) == lax.broadcasted_iota(
             jnp.int32, (length, length), 1
         )
@@ -221,11 +226,11 @@
         rows = rows_of(mb)
 
         def body(n, carry):
-            cols = ds(n * TILE, TILE)
+            cols = ds(n * 3 * TILE, 3 * TILE)
             qkv[rows, cols] = (dot(a[rows, :], wt[:, cols]) + prm[pl.ds(8, 1), cols]).astype(BF16)
             return carry
 
-        lax.fori_loop(0, 3 * width // TILE, body, 0)
+        lax.fori_loop(0, width // TILE, body, 0)
 
     def two_heads(values):
         zero = jnp.zeros_like(values)
@@ -237,7 +242,7 @@
     def attend(mb):
         rows = rows_of(mb)
 
-        def body(p, carry):
+        def one(p):
             q = qkv[rows, ds(p * 128, 128)] * SCALE
             k = qkv[rows, ds(width + p * 128, 128)]
             v = qkv[rows, ds(2 * width + p * 128, 128)]
@@ -245,12 +250,17 @@
             top = jnp.max(s, axis=0, keepdims=True)
             e = jnp.exp(s - top)
             total = jnp.sum(e, axis=0, keepdims=True)
-            lse[mb, p] = top + jnp.log(total)
             prob = (e * (1.0 / total)).astype(BF16)
-            o[rows, ds(p * 128, 128)] = merged(tn_dot(prob, v)).astype(BF16)
-            return carry
-
-        lax.fori_loop(0, pairs, body, 0)
+            return top + jnp.log(total), merged(tn_dot(prob, v)).astype(BF16)
+
+        def body(i, carry):
+            found = [one(i * PAIRS + b) for b in range(PAIRS)]
+            for b, (level, value) in enumerate(found):
+                lse[mb, i * PAIRS + b] = level
+                o[rows, ds((i * PAIRS + b) * 128, 128)] = value
+            return carry
+
+        lax.fori_loop(0, pairs // PAIRS, body, 0)
 
     def project(mb):
         rows = rows_of(mb)
@@ -277,14 +287,14 @@
         rows = rows_of(mb)
 
         def body(n, carry):
-            cols = ds(n * TILE, TILE)
+            cols = ds(n * WIDE, WIDE)
             u = dot(c[rows, :], wu[:, cols]) + prm[pl.ds(9, 1), cols]
             value, slope = gelu_pair(u)
             h[rows, cols] = value.astype(BF16)
             gp[rows, cols] = slope.astype(BF16)
             return carry
 
-        lax.fori_loop(0, feed // TILE, body, 0)
+        lax.fori_loop(0, feed // WIDE, body, 0)
 
     def down(mb):
         rows = rows_of(mb)
@@ -362,13 +372,13 @@
         rows = rows_of(mb)
 
         def body(n, carry):
-            cols = ds(n * TILE, TILE)
+            cols = ds(n * WIDE, WIDE)
             value = (nt_dot(f[rows, :], wd[cols, :]) * gp[rows, cols].astype(F32)).astype(BF16)
             gp[rows, cols] = value
             acc_f[:, cols] += folded(value.astype(F32))
             return carry
 
-        lax.fori_loop(0, feed // TILE, body, 0)
+        lax.fori_loop(0, feed // WIDE, body, 0)
 
     def grad_m(mb):
         rows = rows_of(mb)
@@ -415,7 +425,7 @@
     def grad_attend(mb):
         rows = rows_of(mb)
 
-        def body(p, carry):
+        def one(p):
             qc, kc, vc = (ds(part * width + p * 128, 128) for part in range(3))
             q = two_heads(qkv[rows, qc] * SCALE)
             do = two_heads(g[rows, qc])
@@ -427,14 +437,19 @@
             grad = (prob * (dp - inner)).astype(BF16)
             dk = dot(grad, q).astype(BF16)
             dq = (merged(tn_dot(grad, k)) * SCALE).astype(BF16)
-            qkv[rows, qc] = dq
-            qkv[rows, kc] = dk
-            qkv[rows, vc] = dv
-            acc_t[:, qc] += folded(dq.astype(F32))
-            acc_t[:, vc] += folded(dv.astype(F32))
-            return carry
-
-        lax.fori_loop(0, pairs, body, 0)
+            return dq, dk, dv
+
+        def body(i, carry):
+            found = [one(i * BACK_PAIRS + b) for b in range(BACK_PAIRS)]
+            for b, grads in enumerate(found):
+                for part, value in enumerate(grads):
+                    cols = ds(part * width + (i * BACK_PAIRS + b) * 128, 128)
+                    qkv[rows, cols] = value
+                    if part != 1:
+                        acc_t[:, cols] += folded(value.astype(F32))
+            return carry
+
+        lax.fori_loop(0, pairs // BACK_PAIRS, body, 0)
 
     def grad_x(mb):
         rows = rows_of(mb)
@@ -775,38 +790,77 @@
             returned(i).wait_send()
 
 
-def widen_kernel(per, source, gwd, gwu, gwo, gwt):
-    block = pl.program_id(0)
-    for target, first, after in ((gwd, 0, per), (gwu, per, 2 * per), (gwo, 2 * per, 2 * per + 1), (gwt, 2 * per + 1, 2 * per + 4)):
-
-        @pl.when((block >= first) & (block < after))
-        def _():
-            target[...] = source[...].astype(F32)
-
-
-def widened(blocks, width, per):
-    def beside(first, number):
-        return lambda i: (0, jnp.clip(i - first, 0, number - 1))
-
-    shape = (width, width)
+def widen_kernel(per, width, feed, depth, source, vec, gwd, gwu, gwo, gwt, *rest):
+    vectors, (inside, outside, in_sem, out_sem) = rest[:10], rest[10:]
+    half = width // 2
+    targets = []
+    for block in range(2 * per + 4):
+        for part in range(2):
+            rows = pl.ds(part * half, half)
+            if block < per:
+                targets.append(gwd.at[pl.ds(block * width + part * half, half)])
+            elif block < 2 * per:
+                targets.append(gwu.at[rows, pl.ds((block - per) * width, width)])
+            elif block == 2 * per:
+                targets.append(gwo.at[rows])
+            else:
+                targets.append(gwt.at[rows, pl.ds((block - 2 * per - 1) * width, width)])
+
+    def load(index):
+        slot = index % depth
+        return pltpu.make_async_copy(source.at[pl.ds(index * half, half)], inside.at[slot], in_sem.at[slot])
+
+    def store(index):
+        slot = index % depth
+        return pltpu.make_async_copy(outside.at[slot], targets[index], out_sem.at[slot])
+
+    count = len(targets)
+    for index in range(depth):
+        load(index).start()
+    at = 0
+    for target in vectors:
+        for i in range(target.shape[1] // 128):
+            if target.shape[1] == 2 * width and i == width // 128:
+                at += width // 128
+            target[:, pl.ds(i * 128, 128)] = vec[pl.ds(at, 1), :]
+            at += 1
+    for index in range(count):
+        slot = index % depth
+        load(index).wait()
+        if index >= depth:
+            store(index - depth).wait()
+        outside[slot] = inside[slot].astype(F32)
+        store(index).start()
+        if index + depth < count:
+            load(index + depth).start()
+    for index in range(count - depth, count):
+        store(index).wait()
+
+
+def widened(blocks, vec, width, feed):
+    per, depth = feed // width, 6
+    any_spec = pl.BlockSpec(memory_space=pl.ANY)
+    vmem = pl.BlockSpec(memory_space=pltpu.VMEM)
+    sizes = [width] * 8 + [2 * width, feed]
     return pl.pallas_call(
-        functools.partial(widen_kernel, per),
-        grid=(2 * per + 4,),
-        in_specs=[pl.BlockSpec(shape, lambda i: (i, 0))],
-        out_specs=(
-            pl.BlockSpec(shape, lambda i: (jnp.minimum(i, per - 1), 0)),
-            pl.BlockSpec(shape, beside(per, per)),
-            pl.BlockSpec(shape, beside(2 * per, 1)),
-            pl.BlockSpec(shape, beside(2 * per + 1, 3)),
-        ),
+        functools.partial(widen_kernel, per, width, feed, depth),
+        in_specs=[any_spec, vmem],
+        out_specs=(any_spec,) * 4 + (vmem,) * len(sizes),
         out_shape=(
             jax.ShapeDtypeStruct((per * width, width), F32),
             jax.ShapeDtypeStruct((width, per * width), F32),
             jax.ShapeDtypeStruct((width, width), F32),
             jax.ShapeDtypeStruct((width, 3 * width), F32),
-        ),
+        )
+        + tuple(jax.ShapeDtypeStruct((1, size), F32) for size in sizes),
+        scratch_shapes=[
+            pltpu.VMEM((depth, width // 2, width), BF16),
+            pltpu.VMEM((depth, width // 2, width), F32),
+            pltpu.SemaphoreType.DMA((depth,)),
+            pltpu.SemaphoreType.DMA((depth,)),
+        ],
         compiler_params=pltpu.CompilerParams(vmem_limit_bytes=60 << 20),
-    )(blocks)
+    )(blocks, vec)
 
 
 def local(
@@ -825,8 +879,6 @@
     pieces = n_blocks // group
     streams = pieces * 2 * (ring - 1)
     chunk = group * half // ring
-    key_code = jnp.where(valid_tokens == 1, segments, -1)[:, :, None]
-    query_code = segments[:, None, :]
     any_spec = pl.BlockSpec(memory_space=pl.ANY)
     vmem = pl.BlockSpec(memory_space=pltpu.VMEM)
     sem = pltpu.SemaphoreType.DMA
@@ -894,26 +946,17 @@
             collective_id=0, has_side_effects=True, vmem_limit_bytes=63 << 20
         ),
     )(
-        block_io[0], key_code, query_code, attention_gain, attention_shift, triple_bias, output_bias,
+        block_io[0], segments, valid_tokens, attention_gain, attention_shift, triple_bias, output_bias,
         attention_scale, feed_gain, feed_shift, up_bias, down_bias, feed_scale,
         triple_weight[0], output_weight[0], up_weight[0], down_weight[0],
     )
-    per = feed // width
-    gwd, gwu, gwo, gwt = widened(blocks, width, per)
-
-    flat = vec.reshape(-1)
-    vectors = []
-    at = 0
-    for size in [width] * 8 + [3 * width, feed]:
-        vectors.append(flat[at : at + size][None])
-        at += size
-    ga, gs, gob, gasc, gfg, gfs, gdb, gfsc, gtb, gub = vectors
+    gwd, gwu, gwo, gwt, ga, gs, gob, gasc, gfg, gfs, gdb, gfsc, gtb, gub = widened(blocks, vec, width, feed)
     return (
         ends[None],
         ga,
         gs,
         gwt[None],
-        jnp.concatenate([gtb[:, :width], gtb[:, 2 * width :]], axis=1),
+        gtb,
         gwo[None],
         gob,
         gasc,

time: 283 us -> 263 us (0.929)
  Pallas kernels: 272 us -> 261 us
  local copies, waits for them, and re-layouts: 8.62 us -> 1.28 us
    pallas_call x1, Pallas kernels: 254 us -> 245 us  [local(): pl.pallas_call(functools.partial(kernel, count, length, width, feed, line...]
    broadcast_in_dim x6 -> x0, local copies, waits for them, and re-layouts: 4.51 us -> none  [the longest x4 2.35 us: local(): vectors.append(flat[at:at + size][None])]
where the time goes in v4:
time: 263 us
  Pallas kernels  261 us (99%)
    pallas_call x1, Pallas kernels, local(): pl.pallas_call(functools.partial(kernel, count, length, width, feed, line...  245 us
    pallas_call x1, Pallas kernels, widened(): pl.pallas_call(functools.partial(widen_kernel, per, width, feed, depth),...  15.5 us

profile of v4, /device:TPU:0, one launch (start us, length us, event | category | flops | bytes accessed | tf_op | source)
XLA Modules:
  0.0 262.9 jit_solution(17878691025164412473)
XLA Ops:
  0.7 245.4 %shard_map.280 = (f32[2,320,768]{2,1,0:T(8,128)}, bf16[9216,768]{1,0:T(8,128)(2,1)}, f32[128,128]{1,0:T(8,128)}) custom-call(bf16[2,320,768]{2,1,0:T(8,128)(2,1)} %bitcast.15, s32[2,320]{1,0:T(2,128)} %segment.1, s32[2,320]{1,0:T(2,128)} %valid.1, bf16[1,768]{1,0:T(2,128)(2,1)} %ag.1, bf16[1,768]{1,0:T(2,128)(2,1)} %ash.1, bf16[1,1536]{1,0:T(2,128)(2,1)} %tb.1, ...), custom_call_target="tpu_custom_call" | custom-call | tf_op jit(solution)/shard_map/pallas_call | solution.py:885
  246.1 0.0 copy-start
  246.1 15.5 %shard_map.281 = (f32[3072,768]{1,0:T(8,128)}, f32[768,3072]{1,0:T(8,128)}, f32[768,768]{1,0:T(8,128)}, f32[768,2304]{1,0:T(8,128)}, f32[1,768]{1,0:T(1,128)}, /...) custom-call(bf16[9216,768]{1,0:T(8,128)(2,1)} %get-tuple-element.33., ...), custom_call_target="tpu_custom_call" | custom-call | tf_op jit(solution)/shard_map/pallas_call | solution.py:845
  261.6 0.0 copy-done
  261.6 1.3 copy.33
Async XLA Ops:
  246.1 15.5 %copy-start = (f32[2,320,768]{2,1,0:T(8,128)S(1)}, f32[2,320,768]{2,1,0:T(8,128)}, u32[]{:S(2)}) copy-start(f32[2,320,768]{2,1,0:T(8,128)} %get-tuple-element.32) | copy-start | bytes 5898244

commit v5 on v4

--- a/solution.py
+++ b/solution.py
@@ -18,6 +18,7 @@
 PAIRS = 6
 BACK_PAIRS = 6
 WIDE = 3072
+STEP = 2
 
 FWD, DF, DU, DM, ATT, DX, WD, WU, WT = range(9)
 
@@ -89,13 +90,15 @@
     return first, second
 
 
-def tick_plan(slots, per_phase):
+def tick_plan(slots, per_phase, turns):
     tick, bases, after, starts = 0, [], [], []
     for phase, unused in slots:
         bases.append(tick)
         if phase in (WD, WU, WT):
-            starts += [tick + i for i in range(per_phase)]
-            tick += per_phase
+            for i in range(per_phase):
+                start = tick + (i + 1) * turns // per_phase - 1
+                starts.append(start + (start + len(starts)) % 2)
+            tick += turns
             after.append(1)
         else:
             after.append(1 if starts and phase != DX else 0)
@@ -160,8 +163,7 @@
         for i in range(count):
             load_x(i).start()
 
-    for copy in weight_copies:
-        copy.start()
+    weight_copies[0].start()
 
     @pl.when(trailing)
     def _():
@@ -209,7 +211,6 @@
         banned = jnp.where(same | own, 0.0, -1000000000.0)
         bias[i] = jnp.concatenate([banned, banned], axis=1).astype(BF16)
 
-    pl.semaphore_wait(barrier, 4)
 
     lane = lax.broadcasted_iota(jnp.int32, (length, 128), 1) < HEAD
 
@@ -324,7 +325,13 @@
             handed(mb).wait_recv()
 
         norm_one(mb)
-        when_first(weight_copies[0].wait)
+
+        @pl.when(mb == 0)
+        def _():
+            weight_copies[0].wait()
+            for copy in weight_copies[1:]:
+                copy.start()
+
         triple(mb)
         attend(mb)
         when_first(weight_copies[1].wait)
@@ -335,6 +342,7 @@
         when_first(weight_copies[3].wait)
 
         down(mb)
+        when_first(lambda: pl.semaphore_wait(barrier, 4))
 
         @pl.when(leading)
         def _():
@@ -491,7 +499,7 @@
     piece_rows = group * half
     chunk = piece_rows // ring
     slots = schedules(count)
-    plans = [tick_plan(entry, pieces // 3) for entry in slots]
+    plans = [tick_plan(entry, pieces // 3, 2 * (feed // width) // STEP) for entry in slots]
 
     def chosen(what, index):
         return jnp.where(leading, picked(plans[0][what], index), picked(plans[1][what], index))
@@ -554,9 +562,9 @@
 
     def weight_grad(phase, source, base):
         def body(i, carry):
-            @pl.when((i > 0) & (lax.rem(i, 2 * group) == 0))
+            @pl.when((i > 0) & (lax.rem(i, STEP) == 0))
             def _():
-                tick(base + i // (2 * group) - 1)
+                tick(base + i // STEP - 1)
 
             half_block(phase * halves + i, source)
             return carry
@@ -652,12 +660,17 @@
 
                 pair_copy(k, d, blocks.at[where_out(k, j), pl.ds(d * half, half)], j).start()
 
+        for d in range(2):
+            pl.when((e > 1) & (e <= ring))(lambda d=d: sum_copy(k, d, e - 2, 0).wait_send())
+            pl.when(e > ring)(lambda d=d: all_copy(k, d, e - ring - 1, 0).wait_send())
+
     events = 2 * ring - 1
 
     def tick(t):
         def body(k, carry):
-            e = t - chosen(2, k)
-            pl.when((e >= 0) & (e < events))(lambda: piece_event(k, e))
+            since = t - chosen(2, k)
+            e = since // 2
+            pl.when((since >= 0) & (since % 2 == 0) & (e < events))(lambda: piece_event(k, e))
             return carry
 
         lax.fori_loop(0, pieces, body, 0)
@@ -734,12 +747,8 @@
                 remote(whole, whole, pair_send.at[index], pair_recv.at[index], sibling).wait()
                 own_copy(k, d, 0).wait()
 
-                def sends(s, inner):
-                    sum_copy(k, d, s, 0).wait_send()
-                    all_copy(k, d, s, 0).wait_send()
-                    return inner
-
-                return lax.fori_loop(0, ring - 1, sends, carry)
+                all_copy(k, d, ring - 2, 0).wait_send()
+                return carry
 
             lax.fori_loop(0, pieces, body, 0)
 
@@ -763,7 +772,7 @@
             pl.when(phase == which)(functools.partial(act, mb))
         for number, (which, source) in enumerate(((WD, from_down), (WU, from_up), (WT, from_rest))):
             pl.when(phase == which)(functools.partial(weight_grad, number, source, base))
-        inner = jnp.where(phase >= WD, pieces // 3 - 1, 0)
+        inner = jnp.where(phase >= WD, halves // STEP - 1, 0)
         pl.when(chosen(1, slot) == 1)(lambda: tick(base + inner))
         return carry
 
@@ -774,10 +783,10 @@
     def drain(i, carry):
         t = start + i
         tick(t)
-        pl.when(i < events)(lambda: vector_event(i))
+        pl.when(i % 2 == 0)(lambda: vector_event(i // 2))
         return carry
 
-    lax.fori_loop(0, events, drain, 0)
+    lax.fori_loop(0, 2 * events, drain, 0)
     finish()
 
     @pl.when(leading)

time: 263 us -> 262 us (level)
  no operation moved by 1% of the time
where the time goes in v5:
time: 262 us
  Pallas kernels  260 us (99%)
    pallas_call x1, Pallas kernels, local(): pl.pallas_call(functools.partial(kernel, count, length, width, feed, line...  245 us
    pallas_call x1, Pallas kernels, widened(): pl.pallas_call(functools.partial(widen_kernel, per, width, feed, depth),...  15.5 us

profile of v5, /device:TPU:0, one launch (start us, length us, event | category | flops | bytes accessed | tf_op | source)
XLA Modules:
  0.0 262.0 jit_solution(13807183972221207016)
XLA Ops:
  0.7 244.6 %shard_map.280 = (f32[2,320,768]{2,1,0:T(8,128)}, bf16[9216,768]{1,0:T(8,128)(2,1)}, f32[128,128]{1,0:T(8,128)}) custom-call(bf16[2,320,768]{2,1,0:T(8,128)(2,1)} %bitcast.15, s32[2,320]{1,0:T(2,128)} %segment.1, s32[2,320]{1,0:T(2,128)} %valid.1, bf16[1,768]{1,0:T(2,128)(2,1)} %ag.1, bf16[1,768]{1,0:T(2,128)(2,1)} %ash.1, bf16[1,1536]{1,0:T(2,128)(2,1)} %tb.1, ...), custom_call_target="tpu_custom_call" | custom-call | tf_op jit(solution)/shard_map/pallas_call | solution.py:894
  245.2 0.0 copy-start
  245.2 15.5 %shard_map.281 = (f32[3072,768]{1,0:T(8,128)}, f32[768,3072]{1,0:T(8,128)}, f32[768,768]{1,0:T(8,128)}, f32[768,2304]{1,0:T(8,128)}, f32[1,768]{1,0:T(1,128)}, /...) custom-call(bf16[9216,768]{1,0:T(8,128)(2,1)} %get-tuple-element.33., ...), custom_call_target="tpu_custom_call" | custom-call | tf_op jit(solution)/shard_map/pallas_call | solution.py:854
  260.7 0.0 copy-done
  260.7 1.3 copy.33
Async XLA Ops:
  245.2 15.5 %copy-start = (f32[2,320,768]{2,1,0:T(8,128)S(1)}, f32[2,320,768]{2,1,0:T(8,128)}, u32[]{:S(2)}) copy-start(f32[2,320,768]{2,1,0:T(8,128)} %get-tuple-element.32) | copy-start | bytes 5898244
